TPU v7x, 32 devices: a whole 2x2x4 slice. The times are simulated.
32 devices in a mesh: ctx: 8 (over y, x, core), tp: 4 (over z).
Axes of the slice: x: 2, y: 2, z: 4, core: 2. Of those that a mesh axis runs over, the one named last changes fastest.
Arguments:
- patches: bfloat16 [4096, 1280], P('ctx'), may hold values from -21 to 21
- window_ids: int32 [4096], P('ctx'), may hold values from -1 to 1023, as said below
- positions: int32 [1024], P('ctx'), may hold values from 0 to 8192, as said below
- text_embed: bfloat16 [8192, 8192], P('ctx', 'tp'), may hold values from -6 to 6
- cotangent: bfloat16 [8192, 8192], P('ctx', 'tp'), may hold values from -0.119628906 to 0.119628906
- qkv_weight: bfloat16 [3, 1280, 1280], P(None, None, 'tp'), may hold values from -0.15625 to 0.15625
- out_weight: bfloat16 [1280, 1280], P('tp'), may hold values from -0.15625 to 0.15625
- merger_weight: bfloat16 [5120, 8192], P('ctx', 'tp'), may hold values from -0.078125 to 0.078125
- norm_gain: bfloat16 [8192], P('tp'), may hold values from 0.099609375 to 1.8984375
Outputs:
- normed: bfloat16 [8192, 8192], P('ctx', 'tp')
- merger_grad: float32 [5120, 8192], P('ctx', 'tp')
Inputs may be any that keep to these rules, and one draw needn't show every extreme that they name: `window_ids`: windows are runs of consecutive patch slots of one index of ctx, each of 4 to 64 slots and a multiple of 4; every window id belongs to one index of ctx; the padding slots of an index of ctx come after its live slots and carry -1. Merged slot j of an index of ctx covers its patch slots 4j to 4j+3 and is live exactly when those are; live slots carry distinct positions, dead ones carry 8192. The live slots of one index of ctx name at most 16 positions among the 1024 positions of any one index of ctx.
All inputs are finite; a program needn't handle non-finite values.
Results may differ from a plain program's by a relative error of at most 0.014.
Values may be sent and summed in bfloat16 or wider, within the bound.
No kernel may reach another device: no remote copies, remote signals or barrier semaphores. Data moves between devices by JAX's collectives and lax.ppermute only.
A program may use at most 128 MiB of HBM per device.

v0:
```python
import functools

import jax
import jax.numpy as jnp
from jax import lax
from jax.experimental import pallas as pl
from jax.experimental.pallas import tpu as pltpu
from jax.sharding import PartitionSpec as P


D = 8192
HEAD_DIM = 80
BF = jnp.bfloat16
F32 = jnp.float32


def dot(a, b):
    return jnp.dot(a, b, preferred_element_type=F32)


def contract_rows(left, right):
    return lax.dot_general(left, right, (((0,), (0,)), ((), ())), preferred_element_type=F32)


def swap(x, axis, mask):
    size = lax.axis_size(axis)
    return lax.ppermute(x, axis, [(i, i ^ mask) for i in range(size)])


def nt(a, b):
    return lax.dot_general(a, b, (((1,), (1,)), ((), ())), preferred_element_type=F32)


def log2(size):
    assert size & (size - 1) == 0
    return size.bit_length() - 1


def as_column(row):
    size = row.shape[1]
    eye = lax.broadcasted_iota(jnp.int32, (size, size), 0) == lax.broadcasted_iota(jnp.int32, (size, size), 1)
    return jnp.sum(jnp.where(eye, row.astype(F32), 0.0), axis=1, keepdims=True)


EXTRA = 8


def attention_kernel(n, group, tok_rows, me, positions, ids, patches_hbm, qkv_hbm, *refs):
    outs, residual, (patches, qkv, attended, sems) = refs[:n], refs[n:-4], refs[-4:]
    steps = 4
    size = patches.shape[0] // steps
    copies = [
        pltpu.make_async_copy(patches_hbm.at[pl.ds(i * size, size)], patches.at[pl.ds(i * size, size)], sems.at[i])
        for i in range(steps)
    ]
    size = qkv.shape[1] // 2
    copies += [
        pltpu.make_async_copy(
            qkv_hbm.at[i, pl.ds(j * size, size)], qkv.at[i, pl.ds(j * size, size)], sems.at[steps + 2 * i + j]
        )
        for i in range(3)
        for j in range(2)
    ]
    for copy in copies:
        copy.start()
    c = me[0]
    slots, rows = positions.shape[1], ids.shape[1]
    chips, cap, share = n // 2, slots // n, n // 2 // group

    place = positions[...]
    target = jnp.zeros_like(place)
    for i in range(1, n + 1):
        target = target + (place >= i * tok_rows).astype(jnp.int32)
    earlier = lax.broadcasted_iota(jnp.int32, (slots, slots), 0) < lax.broadcasted_iota(jnp.int32, (slots, slots), 1)
    same = as_column(target) == target.astype(F32)
    rank = jnp.sum(jnp.where(earlier & same, 1.0, 0.0), axis=0, keepdims=True).astype(jnp.int32)
    key = jnp.where(target < n, target * cap + rank, -1)

    per = chips * cap
    row = lax.broadcasted_iota(jnp.int32, (n * per, 1), 0)
    receiver = c ^ (row >> log2(per))
    chip = receiver >> 1
    wanted = (((chip ^ ((row & (per - 1)) >> log2(cap))) * 2 + (receiver & 1)) << log2(cap)) + (row & (cap - 1))
    slot_pick = (wanted == key).astype(BF)
    spread = lax.broadcasted_iota(jnp.int32, (slots, rows), 0) == (
        lax.broadcasted_iota(jnp.int32, (slots, rows), 1) >> log2(group)
    )
    offset = chip >> log2(share) == (lax.broadcasted_iota(jnp.int32, (1, rows), 1) & (group - 1))
    select = jnp.where(offset, dot(slot_pick, spread.astype(BF)), 0.0).astype(BF)

    ids_row = ids[...]
    ids_col = as_column(ids_row)
    allowed = (ids_col == ids_row.astype(F32)) & (ids_col >= 0)
    local = (place - target * tok_rows).astype(F32)
    high_digit = jnp.floor(local * (1.0 / 128))
    digits = jnp.concatenate([high_digit, local - high_digit * 128, jnp.zeros((EXTRA - 2, slots), F32)], axis=0)
    taken = jnp.concatenate([slot_pick[i * per : i * per + cap] for i in range(n)], axis=0)
    numbers = nt(digits.astype(BF), taken)
    filled = nt(jnp.ones((EXTRA, slots), BF), taken)
    numbers = jnp.where(filled > 0, numbers, -1.0)
    for copy in copies[:steps]:
        copy.wait()
    x = patches[...]
    heads = []
    for i in range(3):
        for copy in copies[steps + 2 * i : steps + 2 * i + 2]:
            copy.wait()
        heads.append(nt(qkv[i], x).astype(BF))
    q, k, v = heads
    width = qkv.shape[1]
    for h in range(width // HEAD_DIM):
        part = slice(h * HEAD_DIM, (h + 1) * HEAD_DIM)
        scores = lax.dot_general(k[part], q[part], (((0,), (0,)), ((), ())), preferred_element_type=F32)
        scores = jnp.where(allowed, scores * (1.0 / HEAD_DIM**0.5), F32(-1e30))
        weights = jnp.exp(scores - jnp.max(scores, axis=0, keepdims=True))
        total = jnp.sum(weights, axis=0, keepdims=True)
        attended[part] = (dot(v[part], weights.astype(BF)) / total).astype(BF)
    att = attended[...]
    main = width // 128 * 128
    head, tail = att[:main], att[main:]
    no_head, no_tail = jnp.zeros_like(head), jnp.zeros_like(tail)
    left = jnp.concatenate([head, no_head, tail, no_tail], axis=0)
    right = jnp.concatenate([no_head, head, no_tail, tail], axis=0)
    half = per // 2
    for i in range(n):
        low, high = select[i * per : i * per + half], select[i * per + half : (i + 1) * per]
        outs[i][...] = (nt(low, left) + nt(high, right)).astype(BF)

    if share > 1:
        residual[0][...] = dot(select, x).astype(BF)
        residual[1][...] = numbers.astype(BF)
        return
    picked = dot(select, x).astype(BF)
    blank = jnp.zeros((EXTRA, picked.shape[1] - cap), F32)
    for i in range(n):
        residual[i][:per] = picked[i * per : (i + 1) * per]
        tail = jnp.concatenate([numbers[:, i * cap : (i + 1) * cap], blank], axis=1)
        residual[i][per:] = tail.astype(BF)


def attention(patches, window_ids, positions, qkv_weight, c, n, group, tok_rows):
    rows, dv = patches.shape
    slots, width = positions.shape[0], qkv_weight.shape[2]
    per = n // 2 * (slots // n)
    vmem, hbm = pl.BlockSpec(memory_space=pltpu.VMEM), pl.BlockSpec(memory_space=pltpu.HBM)
    if n // 2 // group > 1:
        extra = [jax.ShapeDtypeStruct((n * per, dv), BF), jax.ShapeDtypeStruct((EXTRA, slots), BF)]
    else:
        extra = [jax.ShapeDtypeStruct((per + EXTRA, dv), BF)] * n
    outs = pl.pallas_call(
        functools.partial(attention_kernel, n, group, tok_rows),
        in_specs=[pl.BlockSpec(memory_space=pltpu.SMEM), vmem, vmem, hbm, hbm],
        out_specs=[vmem] * (n + len(extra)),
        out_shape=[jax.ShapeDtypeStruct((per // 2, 2 * width), BF)] * n + extra,
        scratch_shapes=[
            pltpu.VMEM((rows, dv), BF),
            pltpu.VMEM((3, width, dv), BF),
            pltpu.VMEM((width, rows), BF),
            pltpu.SemaphoreType.DMA((10,)),
        ],
        compiler_params=pltpu.CompilerParams(vmem_limit_bytes=61 * 1024 * 1024),
        name="attention",
    )(c.reshape(1), positions[None, :], window_ids[None, :], patches, jnp.swapaxes(qkv_weight, 1, 2))
    return outs[:n], outs[n:]


def stack_kernel(*refs):
    size = refs[0].shape[0]
    for i, ref in enumerate(refs[:-1]):
        refs[-1][i * size : (i + 1) * size] = ref[...]


def stack_rows(blocks):
    rows, cols = blocks[0].shape
    out = jax.ShapeDtypeStruct((len(blocks) * rows, cols), blocks[0].dtype)
    return pl.pallas_call(
        stack_kernel,
        out_shape=out,
        compiler_params=pltpu.CompilerParams(vmem_limit_bytes=4 * 1024 * 1024),
        name="stack_rows",
    )(*blocks)


def project_kernel(n, cap, size, count_pieces, me, *refs):
    refs = list(refs)

    def take(count):
        got = refs[:count]
        del refs[:count]
        return got

    c, t = me[0], me[1]
    chips = n // 2
    half = chips // 2
    slots = n * cap
    atts = take(size + 1 if size == 4 else size)
    pieces = [take(count_pieces), take(count_pieces)]
    patch, merger = take(n), take(2)
    outs, sends, (numbers,) = take(2), take(2), take(1)
    arranged, low, high, hidden, weights, sems = take(6)
    copies = [pltpu.make_async_copy(merger[i], weights.at[i], sems.at[i]) for i in range(2)]
    for copy in copies:
        copy.start()
    piece_rows, cols = pieces[0][0].shape[1:]
    width = count_pieces * piece_rows
    main = width // 128 * 128
    tail = width - main
    core, chip = c & 1, c >> 1
    at = [core * 2 + (chip >> log2(half)), core * 2 + (chip & 1)]
    if count_pieces == 2:
        at = [core, core]
    for side in range(2):
        for place in range(count_pieces):

            def put(side=side, place=place):
                for k in range(count_pieces):
                    start = (place ^ k) * piece_rows
                    for r in range(size):
                        block = pieces[side][k][r]
                        low[side, r, start : start + piece_rows] = block
                        split = min(max(main - start, 0), piece_rows)
                        if split > 0:
                            high[side, r, start : start + split] = block[:split]
                        if split < piece_rows:
                            high[side, r, start + split + tail : start + piece_rows + tail] = block[split:]

            if count_pieces == 1:
                put()
            else:
                pl.when(at[side] == place)(put)
        for r in range(size):
            low[side, r, width:] = jnp.zeros((tail, cols), BF)
            high[side, r, main : main + tail] = jnp.zeros((tail, cols), BF)

    def arrange(r, ref):
        for j in range(half):
            for p in range(n):
                s, to = p ^ (2 * j), (j * n + p) * cap
                arranged[r, to : to + cap] = ref[(s * half + j) * cap : (s * half + j + 1) * cap]

    for r in range(min(size, len(atts) - 1) if size == 4 else size):
        arrange(r, atts[r])
    if size == 4:
        at_end = (t == 0) | (t == size - 1)

        @pl.when(at_end)
        def _():
            arrange(size - 1, atts[size - 1])

        @pl.when(jnp.logical_not(at_end))
        def _():
            arrange(size - 1, atts[size])

    for s in range(n):
        digits = patch[s][chips * cap :, :cap].astype(F32)
        numbers[s : s + 1, :cap] = digits[0:1] * 128 + digits[1:2]
    for side in range(2):
        for h in range(2):
            base = jnp.concatenate(
                [
                    patch[p ^ (2 * j)][(h * half + j) * cap : (h * half + j + 1) * cap, side * cols : (side + 1) * cols]
                    for j in range(half)
                    for p in range(n)
                ],
                axis=0,
            )
            total = base.astype(F32)
            for r in range(size):
                left = jnp.concatenate([arranged[r, :, h * main : (h + 1) * main], arranged[r, :, 2 * main :]], axis=1)
                total = total + dot(left, (low, high)[h][side, r])
            turn = n // 2 * cap if h else 0
            for j in range(half):
                block = total[j * slots : (j + 1) * slots].astype(BF)
                row = (h * half + j) * slots
                if turn:
                    hidden[side, row : row + turn] = block[turn:]
                    hidden[side, row + turn : row + slots] = block[:turn]
                else:
                    hidden[side, row : row + slots] = block
    for copy in copies:
        copy.wait()
    wide = weights.shape[2] // 2
    for own in range(2):

        @pl.when(core == own)
        def _():
            for i, bit in enumerate((1, chips // 2)):
                ids = [r for r in range(chips) if r & bit]
                total = None
                for side in range(2):
                    left = jnp.concatenate([hidden[side, r * slots : (r + 1) * slots] for r in ids], axis=0)
                    part = dot(left, weights[side ^ own, :, i * wide : (i + 1) * wide])
                    total = part if total is None else total + part
                sends[i][...] = total.astype(BF)
            outs[0][...] = hidden[own]
            outs[1][...] = hidden[1 - own]


def project(c, t, atts, pieces, patch, merger, n, cap, size):
    rows = n // 2 * n * cap
    piece_rows, cols = pieces[0][0].shape[1:]
    width = len(pieces[0]) * piece_rows
    deep = 2 * width - width // 128 * 128
    features = merger[0].shape[1]
    vmem, hbm = pl.BlockSpec(memory_space=pltpu.VMEM), pl.BlockSpec(memory_space=pltpu.HBM)
    args = [*atts, *pieces[0], *pieces[1], *patch]
    out_shape = [jax.ShapeDtypeStruct((rows, cols), BF)] * 2
    out_shape += [jax.ShapeDtypeStruct((rows // 2, features // 2), BF)] * 2
    out_shape += [jax.ShapeDtypeStruct((n, 128), F32)]
    return pl.pallas_call(
        functools.partial(project_kernel, n, cap, size, len(pieces[0])),
        in_specs=[pl.BlockSpec(memory_space=pltpu.SMEM)] + [vmem] * len(args) + [hbm, hbm],
        out_specs=[vmem] * len(out_shape),
        out_shape=out_shape,
        scratch_shapes=[
            pltpu.VMEM((size, rows // 2, 2 * width), BF),
            pltpu.VMEM((2, size, deep, cols), BF),
            pltpu.VMEM((2, size, deep, cols), BF),
            pltpu.VMEM((2, rows, cols), BF),
            pltpu.VMEM((2, cols, features), BF),
            pltpu.SemaphoreType.DMA((2,)),
        ],
        compiler_params=pltpu.CompilerParams(vmem_limit_bytes=40 * 1024 * 1024),
        name="project",
    )(jnp.stack([c, t]), *args, *merger)


def columns_kernel(keys, own, other, *outs):
    for out, ids in zip(outs, keys):
        for i, (ref, key) in enumerate([(ref, key) for ref in (own, other) for key in ids]):
            rows = out.shape[1] // (2 * len(ids))
            block = ref[key * rows : (key + 1) * rows].astype(F32)
            out[:, i * rows : (i + 1) * rows] = block.T.astype(BF)


def turned_columns(own, other, keys, slots):
    return pl.pallas_call(
        functools.partial(columns_kernel, keys),
        out_shape=[jax.ShapeDtypeStruct((own.shape[1], 2 * len(k) * slots), BF) for k in keys],
        compiler_params=pltpu.CompilerParams(vmem_limit_bytes=12 * 1024 * 1024),
        name="turned_columns",
    )(own, other)


def accumulate_kernel(tiles, count, *refs):
    left, right, rest = refs[:2], (refs[2 : 2 + count], refs[2 + count : 2 + 2 * count]), refs[2 + 2 * count :]
    step = pl.program_id(0)
    for i in range(2):

        @pl.when(step // tiles == i)
        def _():
            total = dot(left[i][...], jnp.concatenate([r[...] for r in right[i]], axis=0))
            if len(rest) == 2:
                total = total + rest[0][...]
            rest[-1][...] = total


def accumulate(left, right, total):
    out_rows = left[0].shape[0]
    rows, cols = right[0][0].shape
    count = len(right[0])
    tile = min(cols, 512)
    tiles = cols // tile
    whole = pl.BlockSpec(left[0].shape, lambda i: (0, 0))
    low = pl.BlockSpec((rows, tile), lambda i: (0, jnp.minimum(i, tiles - 1)))
    high = pl.BlockSpec((rows, tile), lambda i: (0, jnp.maximum(i - tiles, 0)))
    across = pl.BlockSpec((out_rows, tile), lambda i: (0, i))
    return pl.pallas_call(
        functools.partial(accumulate_kernel, tiles, count),
        grid=(2 * tiles,),
        in_specs=[whole, whole] + [low] * count + [high] * count + ([] if total is None else [across]),
        out_specs=across,
        out_shape=jax.ShapeDtypeStruct((out_rows, 2 * cols), F32),
        compiler_params=pltpu.CompilerParams(vmem_limit_bytes=20 * 1024 * 1024),
    )(*left, *right[0], *right[1], *([] if total is None else [total]))


def gather_tp(x):
    size = lax.axis_size("tp")
    if size != 4:
        return [x] + [swap(x, "tp", r) for r in range(1, size)]
    far, near = swap(x, "tp", 2), swap(x, "tp", 1)
    x, far = lax.optimization_barrier((x, far))
    ends = lax.ppermute(far, "tp", [(1, 0), (2, 3)])
    middle = lax.ppermute(x, "tp", [(1, 2), (2, 1)])
    return [x, near, far, ends, middle]


def sum_tp(x):
    size = lax.axis_size("tp")
    total = x
    for r in range(1, size):
        total = total + swap(x, "tp", r)
    return total


def shards(
    patches, window_ids, positions, text_embed, cotangent, qkv_weight, out_weight, merger_weight, norm_gain
):
    n = lax.axis_size("ctx")
    tp_size = lax.axis_size("tp")
    chips = n // 2
    c, t = lax.axis_index("ctx"), lax.axis_index("tp")
    chip, core = c // 2, c % 2
    slots, tok_rows = positions.shape[0], text_embed.shape[0]
    features = text_embed.shape[1]
    dv = patches.shape[1]
    own_cols = merger_weight.shape[0]
    group = n * own_cols // dv
    share = chips // group
    cap = slots // n
    ctx_bits = [1 << i for i in range((n - 1).bit_length())]
    chip_bits = ctx_bits[:-1]

    blocks, residual = attention(patches, window_ids, positions, qkv_weight, c, n, group, tok_rows)
    att_mine = stack_rows([blocks[0]] + [swap(blocks[s], "ctx", s) for s in range(1, n)])
    att_all = gather_tp(att_mine)

    width, mid = out_weight.shape[0], dv // 2
    count_pieces = 4 if width % 64 == 0 else 2
    piece_rows = width // count_pieces
    if count_pieces == 4:
        at = [core * 2 + chip // (chips // 2), core * 2 + chip % 2]
    else:
        at = [core, core]
    piece = jnp.concatenate(
        [
            lax.dynamic_slice(out_weight, (at[0] * piece_rows, 0), (piece_rows, mid)),
            lax.dynamic_slice(out_weight, (at[1] * piece_rows, mid), (piece_rows, mid)),
        ],
        axis=1,
    )
    stacked = jnp.stack([piece] + [swap(piece, "tp", r) for r in range(1, tp_size)])
    pieces = []
    for i, bit in enumerate((chips, 2)):
        mine = [stacked[:, :, i * mid : (i + 1) * mid]]
        if count_pieces == 4:
            mine.append(swap(mine[0], "ctx", bit))
        pieces.append(mine + [swap(p, "ctx", 1) for p in mine])

    if share > 1:
        picked, numbers = residual
        picked = picked.reshape(n, chips * cap, dv)
        numbers = jnp.moveaxis(numbers.reshape(EXTRA, n, cap), 1, 0)
        numbers = jnp.concatenate([numbers, jnp.zeros((n, EXTRA, 2 * own_cols - cap), BF)], axis=2)
        residual = [
            jnp.concatenate(
                [
                    lax.dynamic_slice_in_dim(picked[r], ((c ^ r) // 2 % share) * 2 * own_cols, 2 * own_cols, 1),
                    numbers[r],
                ]
            )
            for r in range(n)
        ]
        start = (chip % share) * 2 * own_cols
        full = []
        for i in range(2):
            rows = jnp.stack(pieces[i])
            rows = [lax.dynamic_index_in_dim(rows, q ^ at[i], 0, keepdims=False) for q in range(count_pieces)]
            full.append(jnp.concatenate(rows, axis=1))
        full = jnp.concatenate(full, axis=2)
        pieces = [[lax.dynamic_slice_in_dim(full, start + i * own_cols, own_cols, 2)] for i in range(2)]
    patch = [residual[0]] + [swap(residual[s], "ctx", s) for s in range(1, n)]

    merger = [merger_weight, swap(merger_weight, "ctx", 1)]
    hidden_own, hidden_other, *sends, numbers = project(c, t, att_all, pieces, patch, merger, n, cap, tp_size)
    in_rows = numbers[:, :cap].astype(jnp.int32).reshape(-1)
    placed = jnp.arange(tok_rows, dtype=jnp.int32)[:, None] == in_rows[None, :]
    placed_mat = placed.astype(BF)
    is_vision = jnp.any(placed, axis=1)

    half = features // 2
    arrived = []
    for i, bits in enumerate((chip_bits, chip_bits[::-1])):
        bit = bits[0]
        got = swap(sends[i], "ctx", 2 * bit)
        keep_ids = [r for r in range(chips) if not r & bit]
        keep = 0.0
        for side, weight in ((hidden_own, merger[0]), (hidden_other, merger[1])):
            rows = jnp.concatenate([side[r * slots : (r + 1) * slots] for r in keep_ids])
            keep = keep + dot(rows, weight[:, i * half : (i + 1) * half])
        total = {r: (keep + got.astype(F32)).reshape(-1, slots, half)[k] for k, r in enumerate(keep_ids)}
        for bit in bits[1:]:
            keep_ids = [r for r in total if not r & bit]
            send = jnp.stack([total[r | bit] for r in keep_ids]).astype(BF)
            got = swap(send, "ctx", 2 * bit)
            total = {r: total[r] + got[k].astype(F32) for k, r in enumerate(keep_ids)}
        arrived.append(total[0].astype(BF).astype(F32))

    cot_rows = contract_rows(placed_mat, cotangent).astype(BF)

    gain = norm_gain.astype(F32)[None, :]
    text = text_embed.astype(F32)
    gained = gain * cot_rows
    gained = [gained[:, :half], gained[:, half:]]
    gains = [gain[:, :half], gain[:, half:]]
    squares = sum(jnp.sum(x * x, axis=1) for x in arrived)
    inner = sum(jnp.sum(x * g, axis=1) for x, g in zip(arrived, gained))
    sums = sum_tp(jnp.concatenate([jnp.sum(text * text, axis=1), squares, inner]).reshape(-1, 128)).reshape(-1)
    text_scale = lax.rsqrt(sums[:tok_rows] / D + 1e-06)[:, None]
    scale = lax.rsqrt(sums[tok_rows : tok_rows + slots] / D + 1e-06)[:, None]
    inner = sums[tok_rows + slots :][:, None]
    d_rows = [(scale * g - x * scale**3 * inner / D).astype(BF) for x, g in zip(arrived, gained)]
    rows = jnp.concatenate([(x * scale * g).astype(BF) for x, g in zip(arrived, gains)], axis=1)
    vision = dot(placed_mat, rows)
    normed = jnp.where(is_vision[:, None], vision, text * text_scale * gain).astype(BF)

    blocks = [{0: d_rows[0]}, {0: d_rows[1]}]
    for step in range(len(chip_bits)):
        early = [dict(b) for b in blocks]
        for i, bits in enumerate((chip_bits[::-1], chip_bits)):
            bit = bits[step]
            for k in list(blocks[i]):
                blocks[i][k ^ bit] = swap(blocks[i][k], "ctx", 2 * bit)
    late = [{k: v for k, v in b.items() if k not in e} for b, e in zip(blocks, early)]
    keys = [list(part) for parts in (early, late) for part in parts]
    turned = turned_columns(hidden_own, swap(hidden_other, "ctx", 1), keys, slots)
    merger_grad = None
    for parts, left in ((early, turned[:2]), (late, turned[2:])):
        right = []
        for part in parts:
            mine = list(part.values())
            right.append(mine + [swap(b, "ctx", 1) for b in part.values()])
        merger_grad = accumulate(left, right, merger_grad)
    return (normed, merger_grad)


def solution(mesh):
    in_specs = (
        P("ctx", None),
        P("ctx"),
        P("ctx"),
        P("ctx", "tp"),
        P("ctx", "tp"),
        P(None, None, "tp"),
        P("tp", None),
        P("ctx", "tp"),
        P("tp"),
    )
    out_specs = (P("ctx", "tp"), P("ctx", "tp"))
    return jax.shard_map(shards, mesh=mesh, in_specs=in_specs, out_specs=out_specs, check_vma=False)
```

profile of v0, /device:TPU:0, one launch (start us, length us, event | category | flops | bytes accessed | tf_op | source)
XLA Modules:
  0.0 168.6 jit_solution(4828288910343095437)
XLA Ops:
  1.2 9.9 %attention.1 = (bf16[32,640]{1,0:T(8,128)(2,1)}, bf16[32,640]{1,0:T(8,128)(2,1)}, bf16[32,640]{1,0:T(8,128)(2,1)}, bf16[32,640]{1,0:T(8,128)(2,1)}, bf16[32,640]...) custom-call(s32[1]{0:T(128)} %bitcast.me, ...), custom_call_target="tpu_custom_call" | custom-call | tf_op jit(solution)/shard_map/attention/pallas_call | solution.py:150
  11.2 3.0 %collective-permute-start.1 = (bf16[32,640]{1,0:T(8,128)(2,1)}, bf16[32,640]{1,0:T(8,128)(2,1)S(1)}, u32[]{:S(2)}, u32[]{:S(2)}) collective-permute-start(bf16[32,640]{1,0:T(8,128)(2,1)} %get-tuple-element.31), channel_id=1, source_target_pairs={{0,8},{4,12},{8,0},{12,4},{16,24},{20,28},{24,16},{28,20},{1,9},{5... | collective-permute-start | bytes 122888 | tf_op jit(solution)/shard_map/ppermute | solution.py:27
  17.0 2.7 %collective-permute-start.5 = (bf16[32,640]{1,0:T(8,128)(2,1)}, bf16[32,640]{1,0:T(8,128)(2,1)S(1)}, u32[]{:S(2)}, u32[]{:S(2)}) collective-permute-start(bf16[32,640]{1,0:T(8,128)(2,1)} %get-tuple-element.35), channel_id=1, source_target_pairs={{0,24},{4,28},{8,16},{12,20},{16,8},{20,12},{24,0},{28,4},{1,25},{... | collective-permute-start | bytes 122888 | tf_op jit(solution)/shard_map/ppermute | solution.py:27
  19.7 2.7 %collective-permute-start.12 = (bf16[80,1280]{1,0:T(8,128)(2,1)S(1)}, bf16[80,1280]{1,0:T(8,128)(2,1)S(1)}, u32[]{:S(2)}, u32[]{:S(2)}) collective-permute-start(bf16[80,1280]{1,0:T(8,128)(2,1)S(1)} %get-tuple-element.77), channel_id=1, source_target_pairs={{0,2},{1,3},{2,0},{3,1},{4,6},{5,7},{6,4},{7,5},{8,10},{9,11},{10,... | collective-permute-start | bytes 614408 | tf_op jit(solution)/shard_map/ppermute | solution.py:27
  22.4 1.6 collective-permute-start.11
  24.0 1.9 %collective-permute-start.13 = (bf16[80,1280]{1,0:T(8,128)(2,1)S(1)}, bf16[80,1280]{1,0:T(8,128)(2,1)S(1)}, u32[]{:S(2)}, u32[]{:S(2)}) collective-permute-start(bf16[80,1280]{1,0:T(8,128)(2,1)S(1)} %get-tuple-element.77), channel_id=1, source_target_pairs={{0,3},{1,2},{2,1},{3,0},{4,7},{5,6},{6,5},{7,4},{8,11},{9,10},{10,... | collective-permute-start | bytes 614408 | tf_op jit(solution)/shard_map/ppermute | solution.py:27
  28.2 1.6 collective-permute-start.21
  29.8 3.3 %collective-permute-done.12 = bf16[80,1280]{1,0:T(8,128)(2,1)S(1)} collective-permute-done((bf16[80,1280]{1,0:T(8,128)(2,1)S(1)}, bf16[80,1280]{1,0:T(8,128)(2,1)S(1)}, u32[]{:S(2)}, u32[]{:S(2)}) %collective-permute-start.12) | collective-permute-done | bytes 204832 | tf_op jit(solution)/shard_map/ppermute | solution.py:27
  33.6 1.6 collective-permute-start.23
  35.3 2.9 %collective-permute-done.13 = bf16[80,1280]{1,0:T(8,128)(2,1)S(1)} collective-permute-done((bf16[80,1280]{1,0:T(8,128)(2,1)S(1)}, bf16[80,1280]{1,0:T(8,128)(2,1)S(1)}, u32[]{:S(2)}, u32[]{:S(2)}) %collective-permute-start.13) | collective-permute-done | bytes 204832 | tf_op jit(solution)/shard_map/ppermute | solution.py:27
  39.1 1.7 %collective-permute-start.25 = (bf16[72,1280]{1,0:T(8,128)(2,1)}, bf16[72,1280]{1,0:T(8,128)(2,1)S(1)}, u32[]{:S(2)}, u32[]{:S(2)}) collective-permute-start(bf16[72,1280]{1,0:T(8,128)(2,1)} %get-tuple-element.45), channel_id=1, source_target_pairs={{0,24},{4,28},{8,16},{12,20},{16,8},{20,12},{24,0},{28,4},{1,25},{... | collective-permute-start | bytes 552968 | tf_op jit(solution)/shard_map/ppermute | solution.py:27
  42.2 3.9 %collective-permute-start.8 = (bf16[256,640]{1,0:T(8,128)(2,1)S(1)}, bf16[256,640]{1,0:T(8,128)(2,1)S(1)}, u32[]{:S(2)}, u32[]{:S(2)}) collective-permute-start(bf16[256,640]{1,0:T(8,128)(2,1)S(1)} %stack_rows.1.refs_0_), channel_id=1, source_target_pairs={{0,1},{1,0},{2,3},{3,2},{4,5},{5,4},{6,7},{7,6},{8,9},{9,8},{10,11... | collective-permute-start | bytes 983048 | tf_op jit(solution)/shard_map/ppermute | solution.py:27
  46.2 7.0 %collective-permute-done.24.refs_18_ = bf16[72,1280]{1,0:T(8,128)(2,1)S(1)} collective-permute-done((bf16[72,1280]{1,0:T(8,128)(2,1)}, bf16[72,1280]{1,0:T(8,128)(2,1)S(1)}, u32[]{:S(2)}, u32[]{:S(2)}) %collective-permute-start.24) | collective-permute-done | bytes 184352 | tf_op jit(solution)/shard_map/ppermute | solution.py:27
  53.2 5.6 %collective-permute-start.7 = (bf16[256,640]{1,0:T(8,128)(2,1)S(1)}, bf16[256,640]{1,0:T(8,128)(2,1)S(1)}, u32[]{:S(2)}, u32[]{:S(2)}) collective-permute-start(bf16[256,640]{1,0:T(8,128)(2,1)S(1)} %stack_rows.1.refs_0_), channel_id=1, source_target_pairs={{0,2},{1,3},{2,0},{3,1},{4,6},{5,7},{6,4},{7,5},{8,10},{9,11},{10,... | collective-permute-start | bytes 983048 | tf_op jit(solution)/shard_map/ppermute | solution.py:27
  64.1 9.7 %collective-permute-done.7.refs_2_ = bf16[256,640]{1,0:T(8,128)(2,1)S(1)} collective-permute-done((bf16[256,640]{1,0:T(8,128)(2,1)S(1)}, bf16[256,640]{1,0:T(8,128)(2,1)S(1)}, u32[]{:S(2)}, u32[]{:S(2)}) %collective-permute-start.7) | collective-permute-done | bytes 327712 | tf_op jit(solution)/shard_map/ppermute | solution.py:27
  77.7 3.1 %fusion = f32[1024]{0:T(1024)S(1)} fusion(bf16[1024,2048]{1,0:T(8,128)(2,1)} %param.12), kind=kLoop, calls=%fused_computation.2 | loop fusion | flops 6290432 | bytes 4198400 | tf_op jit(solution)/shard_map/reduce_sum | solution.py:499
  80.8 7.5 %collective-permute-done.9.refs_3_ = bf16[256,640]{1,0:T(8,128)(2,1)S(1)} collective-permute-done((bf16[256,640]{1,0:T(8,128)(2,1)}, bf16[256,640]{1,0:T(8,128)(2,1)S(1)}, u32[]{:S(2)}, u32[]{:S(2)}) %collective-permute-start.9) | collective-permute-done | bytes 327712 | tf_op jit(solution)/shard_map/ppermute | solution.py:384
  95.0 7.7 %project.1 = (bf16[512,640]{1,0:T(8,128)(2,1)S(1)}, bf16[512,640]{1,0:T(8,128)(2,1)S(1)}, bf16[256,1024]{1,0:T(8,128)(2,1)S(1)}, bf16[256,1024]{1,0:T(8,128)(2,1)S(1)}, f32[8,128]{1,0:T(8,128)S(1)}) custom-call(s32[2]{0:T(128)S(1)} %pad_add_fusion.me, bf16[256,640]{1,0:T(8,128)(2,1)S(1)} %copy-done.7, bf16[256,640]{1,0:T(8,128)(2,1)S(1)} %copy-done.11, ...), custom_call_target="tpu_custom_call" | custom-call | tf_op jit(solution)/shard_map/project/pallas_call | solution.py:310
  105.3 1.6 collective-permute-start.28
  109.5 2.0 %fusion.12 = f32[256,1024]{1,0:T(8,128)S(1)} fusion(bf16[640,2048]{1,0:T(8,128)(2,1)} %refs_21_.1, bf16[128,640]{1,0:T(8,128)(2,1)S(1)} %get-tuple-element.80, bf16[128,640]{1,0:T(8,128)(2,1)S(1)} %get-tuple-element.81), kind=kOutput, calls=%fused_computation.17 | convolution fusion | flops 336199680 | bytes 2686976 | tf_op jit(solution)/shard_map/dot_general | solution.py:18
  112.1 7.9 %collective-permute-done.30 = bf16[256,1024]{1,0:T(8,128)(2,1)S(1)} collective-permute-done((bf16[256,1024]{1,0:T(8,128)(2,1)}, bf16[256,1024]{1,0:T(8,128)(2,1)S(1)}, u32[]{:S(2)}, u32[]{:S(2)}) %collective-permute-start.30) | collective-permute-done | bytes 524320 | tf_op jit(solution)/shard_map/ppermute | solution.py:27
  121.3 1.6 collective-permute-start.29
  124.2 3.6 %collective-permute-done.29 = bf16[1,128,1024]{2,1,0:T(8,128)(2,1)S(1)} collective-permute-done((bf16[1,128,1024]{2,1,0:T(8,128)(2,1)S(1)}, bf16[1,128,1024]{2,1,0:T(8,128)(2,1)S(1)}, u32[]{:S(2)}, u32[]{:S(2)}) %collective-permute-start.29) | collective-permute-done | bytes 262176 | tf_op jit(solution)/shard_map/ppermute | solution.py:27
  129.7 2.0 %collective-permute-start.34 = (f32[10,128]{1,0:T(8,128)S(1)}, f32[10,128]{1,0:T(8,128)S(1)}, u32[]{:S(2)}, u32[]{:S(2)}) collective-permute-start(f32[10,128]{1,0:T(8,128)S(1)} %maximum_bitcast_fusion), channel_id=1, source_target_pairs={{0,3},{1,2},{2,1},{3,0},{4,7},{5,6},{6,5},{7,4},{8,11},{9,10},{10,... | collective-permute-start | bytes 15368 | tf_op jit(solution)/shard_map/ppermute | solution.py:27
  138.6 1.6 collective-permute-start.36
  140.3 5.0 %collective-permute-done.42.refs_7_ = bf16[128,1024]{1,0:T(8,128)(2,1)S(1)} collective-permute-done((bf16[128,1024]{1,0:T(8,128)(2,1)S(1)}, bf16[128,1024]{1,0:T(8,128)(2,1)S(1)}, u32[]{:S(2)}, u32[]{:S(2)}) %collective-permute-start.42) | collective-permute-done | bytes 262176 | tf_op jit(solution)/shard_map/ppermute | solution.py:27
  146.3 5.1 %collective-permute-done.37.refs_3_ = bf16[128,1024]{1,0:T(8,128)(2,1)S(1)} collective-permute-done((bf16[128,1024]{1,0:T(8,128)(2,1)S(1)}, bf16[128,1024]{1,0:T(8,128)(2,1)S(1)}, u32[]{:S(2)}, u32[]{:S(2)}) %collective-permute-start.37) | collective-permute-done | bytes 262176 | tf_op jit(solution)/shard_map/ppermute | solution.py:27
  154.6 1.6 collective-permute-done.43.refs_7_
  156.2 1.9 %collective-permute-done.38.refs_3_ = bf16[128,1024]{1,0:T(8,128)(2,1)S(1)} collective-permute-done((bf16[128,1024]{1,0:T(8,128)(2,1)S(1)}, bf16[128,1024]{1,0:T(8,128)(2,1)S(1)}, u32[]{:S(2)}, u32[]{:S(2)}) %collective-permute-start.38) | collective-permute-done | bytes 262176 | tf_op jit(solution)/shard_map/ppermute | solution.py:27
  158.1 3.4 %fusion.3 = bf16[1024,2048]{1,0:T(8,128)(2,1)} fusion(bf16[1024,2048]{1,0:T(8,128)(2,1)S(1)} %copy-done.32, f32[2048]{0:T(1024)S(1)} %convert_element_type.85, f32[1024]{0:T(1024)S(1)} %fusion.50, pred[1024]{0:T(1024)(128)(4,1)S(1)} %fusion.35, bf16[128,1024]{1,0:T(8,128)(2,1)S(1)} %get-tuple-element.75, bf16[128,1024]{1,0:T(8,128)(2,1)S(1)} %get-tuple-element.74, ...), kind=kOutput, calls=%fused_computation.5 | convolution fusion | flops 548536320 | bytes 8926720 | tf_op jit(solution)/shard_map/dot_general | solution.py:18
  161.5 2.8 %shard_map.104.refs_10_ = f32[640,2048]{1,0:T(8,128)S(1)} custom-call(bf16[640,512]{1,0:T(8,128)(2,1)S(1)} %get-tuple-element.54.refs_0_, bf16[640,512]{1,0:T(8,128)(2,1)S(1)} %get-tuple-element.55.refs_1_, bf16[128,1024]{1,0:T(8,128)(2,1)S(1)} %get-tuple-element.65.refs_2_, bf16[128,1024]{1,0:T(8,128)(2,1)S(1)} %collective-permute-done.37.refs_3_, ...), custom_call_target="tpu_custom_call" | custom-call | tf_op jit(solution)/shard_map/pallas_call | solution.py:368
  164.4 4.2 %shard_map.105 = f32[640,2048]{1,0:T(8,128)} custom-call(bf16[640,512]{1,0:T(8,128)(2,1)S(1)} %get-tuple-element.52.refs_0_, bf16[640,512]{1,0:T(8,128)(2,1)S(1)} %get-tuple-element.53.refs_1_, bf16[128,1024]{1,0:T(8,128)(2,1)S(1)} %collective-permute-done.36.refs_2_, bf16[128,1024]{1,0:T(8,128)(2,1)S(1)} %collective-permute-done.38.refs_3_, ...), custom_call_target="tpu_custom_call" | custom-call | tf_op jit(solution)/shard_map/pallas_call | solution.py:368
  (173 shorter events, 45.6 us)
Async XLA Ops:
  0.6 87.7 %collective-permute-start.27 = (bf16[640,2048]{1,0:T(8,128)(2,1)}, bf16[640,2048]{1,0:T(8,128)(2,1)S(1)}, u32[]{:S(2)}, u32[]{:S(2)}) collective-permute-start(bf16[640,2048]{1,0:T(8,128)(2,1)} %refs_21_.1), channel_id=1, source_target_pairs={{0,4},{4,0},{8,12},{12,8},{16,20},{20,16},{24,28},{28,24},{1,5},{5... | collective-permute-start | bytes 7864328 | tf_op jit(solution)/shard_map/ppermute | solution.py:27
  17.0 7.0 %collective-permute-start.5 = (bf16[32,640]{1,0:T(8,128)(2,1)}, bf16[32,640]{1,0:T(8,128)(2,1)S(1)}, u32[]{:S(2)}, u32[]{:S(2)}) collective-permute-start(bf16[32,640]{1,0:T(8,128)(2,1)} %get-tuple-element.35), channel_id=1, source_target_pairs={{0,24},{4,28},{8,16},{12,20},{16,8},{20,12},{24,0},{28,4},{1,25},{... | collective-permute-start | bytes 122888 | tf_op jit(solution)/shard_map/ppermute | solution.py:27
  19.7 13.3 %collective-permute-start.12 = (bf16[80,1280]{1,0:T(8,128)(2,1)S(1)}, bf16[80,1280]{1,0:T(8,128)(2,1)S(1)}, u32[]{:S(2)}, u32[]{:S(2)}) collective-permute-start(bf16[80,1280]{1,0:T(8,128)(2,1)S(1)} %get-tuple-element.77), channel_id=1, source_target_pairs={{0,2},{1,3},{2,0},{3,1},{4,6},{5,7},{6,4},{7,5},{8,10},{9,11},{10,... | collective-permute-start | bytes 614408 | tf_op jit(solution)/shard_map/ppermute | solution.py:27
  22.4 11.2 %collective-permute-start.11 = (bf16[80,1280]{1,0:T(8,128)(2,1)S(1)}, bf16[80,1280]{1,0:T(8,128)(2,1)S(1)}, u32[]{:S(2)}, u32[]{:S(2)}) collective-permute-start(bf16[80,1280]{1,0:T(8,128)(2,1)S(1)} %get-tuple-element.77), channel_id=1, source_target_pairs={{0,1},{1,0},{2,3},{3,2},{4,5},{5,4},{6,7},{7,6},{8,9},{9,8},{10,11... | collective-permute-start | bytes 614408 | tf_op jit(solution)/shard_map/ppermute | solution.py:27
  24.0 14.2 %collective-permute-start.13 = (bf16[80,1280]{1,0:T(8,128)(2,1)S(1)}, bf16[80,1280]{1,0:T(8,128)(2,1)S(1)}, u32[]{:S(2)}, u32[]{:S(2)}) collective-permute-start(bf16[80,1280]{1,0:T(8,128)(2,1)S(1)} %get-tuple-element.77), channel_id=1, source_target_pairs={{0,3},{1,2},{2,1},{3,0},{4,7},{5,6},{6,5},{7,4},{8,11},{9,10},{10,... | collective-permute-start | bytes 614408 | tf_op jit(solution)/shard_map/ppermute | solution.py:27
  28.2 10.9 %collective-permute-start.21 = (bf16[72,1280]{1,0:T(8,128)(2,1)}, bf16[72,1280]{1,0:T(8,128)(2,1)S(1)}, u32[]{:S(2)}, u32[]{:S(2)}) collective-permute-start(bf16[72,1280]{1,0:T(8,128)(2,1)} %get-tuple-element.41), channel_id=1, source_target_pairs={{0,8},{4,12},{8,0},{12,4},{16,24},{20,28},{24,16},{28,20},{1,9},{5... | collective-permute-start | bytes 552968 | tf_op jit(solution)/shard_map/ppermute | solution.py:27
  33.1 7.8 %collective-permute-start.22 = (bf16[72,1280]{1,0:T(8,128)(2,1)}, bf16[72,1280]{1,0:T(8,128)(2,1)S(1)}, u32[]{:S(2)}, u32[]{:S(2)}) collective-permute-start(bf16[72,1280]{1,0:T(8,128)(2,1)} %get-tuple-element.42), channel_id=1, source_target_pairs={{0,12},{4,8},{8,4},{12,0},{16,28},{20,24},{24,20},{28,16},{1,13},{... | collective-permute-start | bytes 552968 | tf_op jit(solution)/shard_map/ppermute | solution.py:27
  33.6 8.6 %collective-permute-start.23 = (bf16[72,1280]{1,0:T(8,128)(2,1)}, bf16[72,1280]{1,0:T(8,128)(2,1)S(1)}, u32[]{:S(2)}, u32[]{:S(2)}) collective-permute-start(bf16[72,1280]{1,0:T(8,128)(2,1)} %get-tuple-element.43), channel_id=1, source_target_pairs={{0,16},{4,20},{8,24},{12,28},{16,0},{20,4},{24,8},{28,12},{1,17},{... | collective-permute-start | bytes 552968 | tf_op jit(solution)/shard_map/ppermute | solution.py:27
  38.2 15.0 %collective-permute-start.24 = (bf16[72,1280]{1,0:T(8,128)(2,1)}, bf16[72,1280]{1,0:T(8,128)(2,1)S(1)}, u32[]{:S(2)}, u32[]{:S(2)}) collective-permute-start(bf16[72,1280]{1,0:T(8,128)(2,1)} %get-tuple-element.44), channel_id=1, source_target_pairs={{0,20},{4,16},{8,28},{12,24},{16,4},{20,0},{24,12},{28,8},{1,21},{... | collective-permute-start | bytes 552968 | tf_op jit(solution)/shard_map/ppermute | solution.py:27
  39.1 19.7 %collective-permute-start.25 = (bf16[72,1280]{1,0:T(8,128)(2,1)}, bf16[72,1280]{1,0:T(8,128)(2,1)S(1)}, u32[]{:S(2)}, u32[]{:S(2)}) collective-permute-start(bf16[72,1280]{1,0:T(8,128)(2,1)} %get-tuple-element.45), channel_id=1, source_target_pairs={{0,24},{4,28},{8,16},{12,20},{16,8},{20,12},{24,0},{28,4},{1,25},{... | collective-permute-start | bytes 552968 | tf_op jit(solution)/shard_map/ppermute | solution.py:27
  40.9 20.3 %collective-permute-start.26 = (bf16[72,1280]{1,0:T(8,128)(2,1)}, bf16[72,1280]{1,0:T(8,128)(2,1)S(1)}, u32[]{:S(2)}, u32[]{:S(2)}) collective-permute-start(bf16[72,1280]{1,0:T(8,128)(2,1)} %get-tuple-element.46), channel_id=1, source_target_pairs={{0,28},{4,24},{8,20},{12,16},{16,12},{20,8},{24,4},{28,0},{1,29},{... | collective-permute-start | bytes 552968 | tf_op jit(solution)/shard_map/ppermute | solution.py:27
  42.2 21.1 %collective-permute-start.8 = (bf16[256,640]{1,0:T(8,128)(2,1)S(1)}, bf16[256,640]{1,0:T(8,128)(2,1)S(1)}, u32[]{:S(2)}, u32[]{:S(2)}) collective-permute-start(bf16[256,640]{1,0:T(8,128)(2,1)S(1)} %stack_rows.1.refs_0_), channel_id=1, source_target_pairs={{0,1},{1,0},{2,3},{3,2},{4,5},{5,4},{6,7},{7,6},{8,9},{9,8},{10,11... | collective-permute-start | bytes 983048 | tf_op jit(solution)/shard_map/ppermute | solution.py:27
  53.2 20.6 %collective-permute-start.7 = (bf16[256,640]{1,0:T(8,128)(2,1)S(1)}, bf16[256,640]{1,0:T(8,128)(2,1)S(1)}, u32[]{:S(2)}, u32[]{:S(2)}) collective-permute-start(bf16[256,640]{1,0:T(8,128)(2,1)S(1)} %stack_rows.1.refs_0_), channel_id=1, source_target_pairs={{0,2},{1,3},{2,0},{3,1},{4,6},{5,7},{6,4},{7,5},{8,10},{9,11},{10,... | collective-permute-start | bytes 983048 | tf_op jit(solution)/shard_map/ppermute | solution.py:27
  59.6 15.0 %collective-permute-start.17 = (bf16[4,80,640]{2,1,0:T(8,128)(2,1)S(1)}, bf16[4,80,640]{2,1,0:T(8,128)(2,1)}, u32[]{:S(2)}, u32[]{:S(2)}) collective-permute-start(bf16[4,80,640]{2,1,0:T(8,128)(2,1)S(1)} %get-tuple-element.66.refs_9_), channel_id=1, source_target_pairs={{0,8},{4,12},{8,0},{12,4},{16,24},{20,28},{24,16},{28,20},{1,9},{5... | collective-permute-start | bytes 1228808 | tf_op jit(solution)/shard_map/ppermute | solution.py:27
  61.8 13.3 %collective-permute-start.14 = (bf16[4,80,640]{2,1,0:T(8,128)(2,1)S(1)}, bf16[4,80,640]{2,1,0:T(8,128)(2,1)}, u32[]{:S(2)}, u32[]{:S(2)}) collective-permute-start(bf16[4,80,640]{2,1,0:T(8,128)(2,1)S(1)} %get-tuple-element.67.refs_5_), channel_id=1, source_target_pairs={{0,16},{4,20},{8,24},{12,28},{16,0},{20,4},{24,8},{28,12},{1,17},{... | collective-permute-start | bytes 1228808 | tf_op jit(solution)/shard_map/ppermute | solution.py:27
  64.1 11.3 %collective-permute-start.18 = (bf16[4,80,640]{2,1,0:T(8,128)(2,1)S(1)}, bf16[4,80,640]{2,1,0:T(8,128)(2,1)}, u32[]{:S(2)}, u32[]{:S(2)}) collective-permute-start(bf16[4,80,640]{2,1,0:T(8,128)(2,1)S(1)} %get-tuple-element.66.refs_9_), channel_id=1, source_target_pairs={{0,4},{4,0},{8,12},{12,8},{16,20},{20,16},{24,28},{28,24},{1,5},{5... | collective-permute-start | bytes 1228808 | tf_op jit(solution)/shard_map/ppermute | solution.py:27
  74.6 13.7 %collective-permute-start.19 = (bf16[4,80,640]{2,1,0:T(8,128)(2,1)}, bf16[4,80,640]{2,1,0:T(8,128)(2,1)S(1)}, u32[]{:S(2)}, u32[]{:S(2)}) collective-permute-start(bf16[4,80,640]{2,1,0:T(8,128)(2,1)} %collective-permute-done.17.refs_10_), channel_id=1, source_target_pairs={{0,4},{4,0},{8,12},{12,8},{16,20},{20,16},{24,28},{28,24},{1,5},{5... | collective-permute-start | bytes 1228808 | tf_op jit(solution)/shard_map/ppermute | solution.py:27
  75.2 13.2 %collective-permute-start.16 = (bf16[4,80,640]{2,1,0:T(8,128)(2,1)}, bf16[4,80,640]{2,1,0:T(8,128)(2,1)S(1)}, u32[]{:S(2)}, u32[]{:S(2)}) collective-permute-start(bf16[4,80,640]{2,1,0:T(8,128)(2,1)} %collective-permute-done.14.refs_6_), channel_id=1, source_target_pairs={{0,4},{4,0},{8,12},{12,8},{16,20},{20,16},{24,28},{28,24},{1,5},{5... | collective-permute-start | bytes 1228808 | tf_op jit(solution)/shard_map/ppermute | solution.py:27
  76.4 11.9 %collective-permute-start.9 = (bf16[256,640]{1,0:T(8,128)(2,1)}, bf16[256,640]{1,0:T(8,128)(2,1)S(1)}, u32[]{:S(2)}, u32[]{:S(2)}) collective-permute-start(bf16[256,640]{1,0:T(8,128)(2,1)} %copy-done.12), channel_id=1, source_target_pairs={{1,0},{2,3},{5,4},{6,7},{9,8},{10,11},{13,12},{14,15},{17,16},{18,... | collective-permute-start | bytes 983048 | tf_op jit(solution)/shard_map/ppermute | solution.py:384
  105.3 15.4 %collective-permute-start.28 = (bf16[256,1024]{1,0:T(8,128)(2,1)}, bf16[256,1024]{1,0:T(8,128)(2,1)S(1)}, u32[]{:S(2)}, u32[]{:S(2)}) collective-permute-start(bf16[256,1024]{1,0:T(8,128)(2,1)} %copy-done.30), channel_id=1, source_target_pairs={{0,8},{4,12},{8,0},{12,4},{16,24},{20,28},{24,16},{28,20},{1,9},{5... | collective-permute-start | bytes 1572872 | tf_op jit(solution)/shard_map/ppermute | solution.py:27
  106.9 13.1 %collective-permute-start.30 = (bf16[256,1024]{1,0:T(8,128)(2,1)}, bf16[256,1024]{1,0:T(8,128)(2,1)S(1)}, u32[]{:S(2)}, u32[]{:S(2)}) collective-permute-start(bf16[256,1024]{1,0:T(8,128)(2,1)} %copy-done.31), channel_id=1, source_target_pairs={{0,16},{4,20},{8,24},{12,28},{16,0},{20,4},{24,8},{28,12},{1,17},{... | collective-permute-start | bytes 1572872 | tf_op jit(solution)/shard_map/ppermute | solution.py:27
  136.1 9.2 %collective-permute-start.42 = (bf16[128,1024]{1,0:T(8,128)(2,1)S(1)}, bf16[128,1024]{1,0:T(8,128)(2,1)S(1)}, u32[]{:S(2)}, u32[]{:S(2)}) collective-permute-start(bf16[128,1024]{1,0:T(8,128)(2,1)S(1)} %get-tuple-element.64.refs_6_), channel_id=1, source_target_pairs={{0,8},{4,12},{8,0},{12,4},{16,24},{20,28},{24,16},{28,20},{1,9},{5... | collective-permute-start | bytes 786440 | tf_op jit(solution)/shard_map/ppermute | solution.py:27
  136.6 9.2 %collective-permute-start.41 = (bf16[128,1024]{1,0:T(8,128)(2,1)S(1)}, bf16[128,1024]{1,0:T(8,128)(2,1)S(1)}, u32[]{:S(2)}, u32[]{:S(2)}) collective-permute-start(bf16[128,1024]{1,0:T(8,128)(2,1)S(1)} %get-tuple-element.64.refs_6_), channel_id=1, source_target_pairs={{0,16},{4,20},{8,24},{12,28},{16,0},{20,4},{24,8},{28,12},{1,17},{... | collective-permute-start | bytes 786440 | tf_op jit(solution)/shard_map/ppermute | solution.py:27
  137.1 14.3 %collective-permute-start.37 = (bf16[128,1024]{1,0:T(8,128)(2,1)S(1)}, bf16[128,1024]{1,0:T(8,128)(2,1)S(1)}, u32[]{:S(2)}, u32[]{:S(2)}) collective-permute-start(bf16[128,1024]{1,0:T(8,128)(2,1)S(1)} %get-tuple-element.65.refs_2_), channel_id=1, source_target_pairs={{0,16},{4,20},{8,24},{12,28},{16,0},{20,4},{24,8},{28,12},{1,17},{... | collective-permute-start | bytes 786440 | tf_op jit(solution)/shard_map/ppermute | solution.py:27
  138.6 15.3 %collective-permute-start.46 = (bf16[128,1024]{1,0:T(8,128)(2,1)S(1)}, bf16[128,1024]{1,0:T(8,128)(2,1)S(1)}, u32[]{:S(2)}, u32[]{:S(2)}) collective-permute-start(bf16[128,1024]{1,0:T(8,128)(2,1)S(1)} %get-tuple-element.65.refs_2_), channel_id=1, source_target_pairs={{0,4},{4,0},{8,12},{12,8},{16,20},{20,16},{24,28},{28,24},{1,5},{5... | collective-permute-start | bytes 786440 | tf_op jit(solution)/shard_map/ppermute | solution.py:27
  138.6 15.4 %collective-permute-start.36 = (bf16[128,1024]{1,0:T(8,128)(2,1)S(1)}, bf16[128,1024]{1,0:T(8,128)(2,1)S(1)}, u32[]{:S(2)}, u32[]{:S(2)}) collective-permute-start(bf16[128,1024]{1,0:T(8,128)(2,1)S(1)} %get-tuple-element.65.refs_2_), channel_id=1, source_target_pairs={{0,8},{4,12},{8,0},{12,4},{16,24},{20,28},{24,16},{28,20},{1,9},{5... | collective-permute-start | bytes 786440 | tf_op jit(solution)/shard_map/ppermute | solution.py:27
  145.3 9.2 %collective-permute-start.49 = (bf16[128,1024]{1,0:T(8,128)(2,1)S(1)}, bf16[128,1024]{1,0:T(8,128)(2,1)S(1)}, u32[]{:S(2)}, u32[]{:S(2)}) collective-permute-start(bf16[128,1024]{1,0:T(8,128)(2,1)S(1)} %collective-permute-done.42.refs_7_), channel_id=1, source_target_pairs={{0,4},{4,0},{8,12},{12,8},{16,20},{20,16},{24,28},{28,24},{1,5},{5... | collective-permute-start | bytes 786440 | tf_op jit(solution)/shard_map/ppermute | solution.py:27
  145.8 10.4 %collective-permute-start.43 = (bf16[128,1024]{1,0:T(8,128)(2,1)S(1)}, bf16[128,1024]{1,0:T(8,128)(2,1)S(1)}, u32[]{:S(2)}, u32[]{:S(2)}) collective-permute-start(bf16[128,1024]{1,0:T(8,128)(2,1)S(1)} %collective-permute-done.42.refs_7_), channel_id=1, source_target_pairs={{0,16},{4,20},{8,24},{12,28},{16,0},{20,4},{24,8},{28,12},{1,17},{... | collective-permute-start | bytes 786440 | tf_op jit(solution)/shard_map/ppermute | solution.py:27
  154.0 7.6 %collective-permute-start.47 = (bf16[128,1024]{1,0:T(8,128)(2,1)S(1)}, bf16[128,1024]{1,0:T(8,128)(2,1)S(1)}, u32[]{:S(2)}, u32[]{:S(2)}) collective-permute-start(bf16[128,1024]{1,0:T(8,128)(2,1)S(1)} %collective-permute-done.37.refs_3_), channel_id=1, source_target_pairs={{0,4},{4,0},{8,12},{12,8},{16,20},{20,16},{24,28},{28,24},{1,5},{5... | collective-permute-start | bytes 786440 | tf_op jit(solution)/shard_map/ppermute | solution.py:27
  154.0 10.3 %collective-permute-start.44 = (bf16[128,1024]{1,0:T(8,128)(2,1)S(1)}, bf16[128,1024]{1,0:T(8,128)(2,1)S(1)}, u32[]{:S(2)}, u32[]{:S(2)}) collective-permute-start(bf16[128,1024]{1,0:T(8,128)(2,1)S(1)} %collective-permute-done.41.refs_6_), channel_id=1, source_target_pairs={{0,4},{4,0},{8,12},{12,8},{16,20},{20,16},{24,28},{28,24},{1,5},{5... | collective-permute-start | bytes 786440 | tf_op jit(solution)/shard_map/ppermute | solution.py:27
  154.5 9.8 %collective-permute-start.39 = (bf16[128,1024]{1,0:T(8,128)(2,1)S(1)}, bf16[128,1024]{1,0:T(8,128)(2,1)S(1)}, u32[]{:S(2)}, u32[]{:S(2)}) collective-permute-start(bf16[128,1024]{1,0:T(8,128)(2,1)S(1)} %collective-permute-done.36.refs_2_), channel_id=1, source_target_pairs={{0,4},{4,0},{8,12},{12,8},{16,20},{20,16},{24,28},{28,24},{1,5},{5... | collective-permute-start | bytes 786440 | tf_op jit(solution)/shard_map/ppermute | solution.py:27
  156.2 8.1 %collective-permute-start.45 = (bf16[128,1024]{1,0:T(8,128)(2,1)S(1)}, bf16[128,1024]{1,0:T(8,128)(2,1)S(1)}, u32[]{:S(2)}, u32[]{:S(2)}) collective-permute-start(bf16[128,1024]{1,0:T(8,128)(2,1)S(1)} %collective-permute-done.43.refs_7_), channel_id=1, source_target_pairs={{0,4},{4,0},{8,12},{12,8},{16,20},{20,16},{24,28},{28,24},{1,5},{5... | collective-permute-start | bytes 786440 | tf_op jit(solution)/shard_map/ppermute | solution.py:27
  (53 other events, 529.9 us)
where the time goes:
time: 169 us
  waiting for transfers between devices  60.8 us (36%)
  starting transfers between devices  53.1 us (31%)
  Pallas kernels  25.3 us (15%)
  local copies, waits for them, and re-layouts  15.7 us (9%)
  matrix products  8.07 us (5%)
  other arithmetic  4.44 us (3%)
    ppermute x48, waiting for transfers between devices, swap(): return lax.ppermute(x, axis, [(i, i ^ mask) for i in range(size)])  53.3 us
    ppermute x48, starting transfers between devices, swap(): return lax.ppermute(x, axis, [(i, i ^ mask) for i in range(size)])  51 us
    unnamed x70, local copies, waits for them, and re-layouts  13.4 us
    pallas_call x1, Pallas kernels, attention(): pl.pallas_call(functools.partial(attention_kernel, n, group, tok_rows), i...  9.88 us
    pallas_call x1, Pallas kernels, project(): pl.pallas_call(functools.partial(project_kernel, n, cap, size, len(pieces...  7.7 us
    ppermute x1, waiting for transfers between devices, gather_tp(): ends = lax.ppermute(far, 'tp', [(1, 0), (2, 3)])  7.53 us
    dot_general x5, matrix products, dot(): return jnp.dot(a, b, preferred_element_type=F32)  7.29 us
    pallas_call x2, Pallas kernels, accumulate(): pl.pallas_call(functools.partial(accumulate_kernel, tiles, count), grid=(...  6.98 us
  transfers between devices with their start and end apart: 50, of which 18 were waited for; matrix products, arithmetic and copies ran while one was open for 8% of the time, Pallas kernels for 8%

commit v1 on v0

--- a/solution.py
+++ b/solution.py
@@ -151,7 +151,9 @@
         functools.partial(attention_kernel, n, group, tok_rows),
         in_specs=[pl.BlockSpec(memory_space=pltpu.SMEM), vmem, vmem, hbm, hbm],
         out_specs=[vmem] * (n + len(extra)),
-        out_shape=[jax.ShapeDtypeStruct((per // 2, 2 * width), BF)] * n + extra,
+        out_shape=[pltpu.VMEM((per // 2, 2 * width), BF)]
+        + [jax.ShapeDtypeStruct((per // 2, 2 * width), BF)] * (n - 1)
+        + extra,
         scratch_shapes=[
             pltpu.VMEM((rows, dv), BF),
             pltpu.VMEM((3, width, dv), BF),
@@ -181,6 +183,10 @@
     )(*blocks)
 
 
+def sent_ids(chips, bit):
+    return [r for r in range(chips) if r & bit][::-1]
+
+
 def project_kernel(n, cap, size, count_pieces, me, *refs):
     refs = list(refs)
 
@@ -196,8 +202,8 @@
     atts = take(size + 1 if size == 4 else size)
     pieces = [take(count_pieces), take(count_pieces)]
     patch, merger = take(n), take(2)
-    outs, sends, (numbers,) = take(2), take(2), take(1)
-    arranged, low, high, hidden, weights, sems = take(6)
+    outs, sends, (numbers,) = take(2), take(chips), take(1)
+    arranged, low, high, hidden, products, weights, sems = take(7)
     copies = [pltpu.make_async_copy(merger[i], weights.at[i], sems.at[i]) for i in range(2)]
     for copy in copies:
         copy.start()
@@ -280,20 +286,33 @@
     for copy in copies:
         copy.wait()
     wide = weights.shape[2] // 2
+    away = [
+        pltpu.make_async_copy(products.at[i, pl.ds(k * slots, slots)], sends[i * half + k], sems.at[2 + i * half + k])
+        for i in range(2)
+        for k in range(half)
+    ]
     for own in range(2):
 
         @pl.when(core == own)
         def _():
+            kept = [pltpu.make_async_copy(hidden.at[own ^ i], outs[i], sems.at[2 + chips + i]) for i in range(2)]
+            for copy in kept:
+                copy.start()
             for i, bit in enumerate((1, chips // 2)):
-                ids = [r for r in range(chips) if r & bit]
+                ids = sent_ids(chips, bit)
                 total = None
                 for side in range(2):
                     left = jnp.concatenate([hidden[side, r * slots : (r + 1) * slots] for r in ids], axis=0)
                     part = dot(left, weights[side ^ own, :, i * wide : (i + 1) * wide])
                     total = part if total is None else total + part
-                sends[i][...] = total.astype(BF)
-            outs[0][...] = hidden[own]
-            outs[1][...] = hidden[1 - own]
+                products[i] = total.astype(BF)
+                for k in range(len(ids)):
+                    away[i * len(ids) + k].start()
+            for copy in kept:
+                copy.wait()
+
+    for copy in away:
+        copy.wait()
 
 
 def project(c, t, atts, pieces, patch, merger, n, cap, size):
@@ -304,23 +323,24 @@
     features = merger[0].shape[1]
     vmem, hbm = pl.BlockSpec(memory_space=pltpu.VMEM), pl.BlockSpec(memory_space=pltpu.HBM)
     args = [*atts, *pieces[0], *pieces[1], *patch]
-    out_shape = [jax.ShapeDtypeStruct((rows, cols), BF)] * 2
-    out_shape += [jax.ShapeDtypeStruct((rows // 2, features // 2), BF)] * 2
+    out_shape = [pltpu.HBM((rows, cols), BF)] * 2
+    out_shape += [pltpu.HBM((n * cap, features // 2), BF)] * (n // 2)
     out_shape += [jax.ShapeDtypeStruct((n, 128), F32)]
     return pl.pallas_call(
         functools.partial(project_kernel, n, cap, size, len(pieces[0])),
         in_specs=[pl.BlockSpec(memory_space=pltpu.SMEM)] + [vmem] * len(args) + [hbm, hbm],
-        out_specs=[vmem] * len(out_shape),
+        out_specs=[hbm] * (len(out_shape) - 1) + [vmem],
         out_shape=out_shape,
         scratch_shapes=[
             pltpu.VMEM((size, rows // 2, 2 * width), BF),
             pltpu.VMEM((2, size, deep, cols), BF),
             pltpu.VMEM((2, size, deep, cols), BF),
             pltpu.VMEM((2, rows, cols), BF),
+            pltpu.VMEM((2, rows // 2, features // 2), BF),
             pltpu.VMEM((2, cols, features), BF),
-            pltpu.SemaphoreType.DMA((2,)),
+            pltpu.SemaphoreType.DMA((4 + n // 2,)),
         ],
-        compiler_params=pltpu.CompilerParams(vmem_limit_bytes=40 * 1024 * 1024),
+        compiler_params=pltpu.CompilerParams(vmem_limit_bytes=24 * 1024 * 1024),
         name="project",
     )(jnp.stack([c, t]), *args, *merger)
 
@@ -351,8 +371,9 @@
         def _():
             total = dot(left[i][...], jnp.concatenate([r[...] for r in right[i]], axis=0))
             if len(rest) == 2:
-                total = total + rest[0][...]
-            rest[-1][...] = total
+                rest[1][...] = total + rest[0][:, pl.ds(pl.multiple_of(step * total.shape[1], 128), total.shape[1])]
+            else:
+                rest[0][:, pl.ds(pl.multiple_of(step * total.shape[1], 128), total.shape[1])] = total
 
 
 def accumulate(left, right, total):
@@ -368,9 +389,9 @@
     return pl.pallas_call(
         functools.partial(accumulate_kernel, tiles, count),
         grid=(2 * tiles,),
-        in_specs=[whole, whole] + [low] * count + [high] * count + ([] if total is None else [across]),
-        out_specs=across,
-        out_shape=jax.ShapeDtypeStruct((out_rows, 2 * cols), F32),
+        in_specs=[whole, whole] + [low] * count + [high] * count + ([] if total is None else [pl.BlockSpec(memory_space=pltpu.VMEM)]),
+        out_specs=pl.BlockSpec(memory_space=pltpu.VMEM) if total is None else across,
+        out_shape=(pltpu.VMEM if total is None else jax.ShapeDtypeStruct)((out_rows, 2 * cols), F32),
         compiler_params=pltpu.CompilerParams(vmem_limit_bytes=20 * 1024 * 1024),
     )(*left, *right[0], *right[1], *([] if total is None else [total]))
 
@@ -473,18 +494,19 @@
     arrived = []
     for i, bits in enumerate((chip_bits, chip_bits[::-1])):
         bit = bits[0]
-        got = swap(sends[i], "ctx", 2 * bit)
+        ids = sent_ids(chips, bit)
+        sent = dict(zip(ids, sends[i * len(ids) : (i + 1) * len(ids)]))
         keep_ids = [r for r in range(chips) if not r & bit]
         keep = 0.0
         for side, weight in ((hidden_own, merger[0]), (hidden_other, merger[1])):
             rows = jnp.concatenate([side[r * slots : (r + 1) * slots] for r in keep_ids])
             keep = keep + dot(rows, weight[:, i * half : (i + 1) * half])
-        total = {r: (keep + got.astype(F32)).reshape(-1, slots, half)[k] for k, r in enumerate(keep_ids)}
-        for bit in bits[1:]:
-            keep_ids = [r for r in total if not r & bit]
-            send = jnp.stack([total[r | bit] for r in keep_ids]).astype(BF)
-            got = swap(send, "ctx", 2 * bit)
-            total = {r: total[r] + got[k].astype(F32) for k, r in enumerate(keep_ids)}
+        total = {r: keep[k * slots : (k + 1) * slots] for k, r in enumerate(keep_ids)}
+        for step, bit in enumerate(bits):
+            if step:
+                sent = {r: total[r].astype(BF) for r in total if r & bit}
+            got = {r ^ bit: swap(v, "ctx", 2 * bit) for r, v in sent.items()}
+            total = {r: total[r] + got[r].astype(F32) for r in got}
         arrived.append(total[0].astype(BF).astype(F32))
 
     cot_rows = contract_rows(placed_mat, cotangent).astype(BF)

time: 169 us -> 164 us (0.970)
  local copies, waits for them, and re-layouts: 15.7 us -> 10.5 us
  starting transfers between devices: 53.1 us -> 55.1 us
    unnamed x70 -> x56, local copies, waits for them, and re-layouts: 13.4 us -> 8.17 us
    ppermute x48 -> x50, starting transfers between devices: 51 us -> 53 us  [swap(): return lax.ppermute(x, axis, [(i, i ^ mask) for i in range(size)])]
    ppermute x48 -> x50, waiting for transfers between devices: 53.3 us -> 51.8 us  [swap(): return lax.ppermute(x, axis, [(i, i ^ mask) for i in range(size)])]
  transfers between devices with their start and end apart: 50 -> 52, of which waited for: 18 -> 19; matrix products, arithmetic and copies ran while one was open for 8% -> 9% of each run, Pallas kernels for 8% -> 8%
where the time goes in v1:
time: 164 us
  waiting for transfers between devices  59.4 us (36%)
  starting transfers between devices  55.1 us (34%)
  Pallas kernels  25.5 us (16%)
  local copies, waits for them, and re-layouts  10.5 us (6%)
  matrix products  7.53 us (5%)
  other arithmetic  4.63 us (3%)
    ppermute x50, starting transfers between devices, swap(): return lax.ppermute(x, axis, [(i, i ^ mask) for i in range(size)])  53 us
    ppermute x50, waiting for transfers between devices, swap(): return lax.ppermute(x, axis, [(i, i ^ mask) for i in range(size)])  51.8 us
    pallas_call x1, Pallas kernels, attention(): pl.pallas_call(functools.partial(attention_kernel, n, group, tok_rows), i...  9.88 us
    pallas_call x1, Pallas kernels, project(): pl.pallas_call(functools.partial(project_kernel, n, cap, size, len(pieces...  8.53 us
    unnamed x56, local copies, waits for them, and re-layouts  8.17 us
    ppermute x1, waiting for transfers between devices, gather_tp(): ends = lax.ppermute(far, 'tp', [(1, 0), (2, 3)])  7.53 us
    dot_general x5, matrix products, dot(): return jnp.dot(a, b, preferred_element_type=F32)  6.75 us
    pallas_call x2, Pallas kernels, accumulate(): pl.pallas_call(functools.partial(accumulate_kernel, tiles, count), grid=(...  6.36 us
  transfers between devices with their start and end apart: 52, of which 19 were waited for; matrix products, arithmetic and copies ran while one was open for 9% of the time, Pallas kernels for 8%

profile of v1, /device:TPU:0, one launch (start us, length us, event | category | flops | bytes accessed | tf_op | source)
XLA Modules:
  0.0 163.9 jit_solution(11772628063236017190)
XLA Ops:
  1.2 9.9 %attention.1 = (bf16[32,640]{1,0:T(8,128)(2,1)S(1)}, bf16[32,640]{1,0:T(8,128)(2,1)}, bf16[32,640]{1,0:T(8,128)(2,1)}, bf16[32,640]{1,0:T(8,128)(2,1)}, bf16[32,...) custom-call(s32[1]{0:T(128)} %bitcast.me, ...), custom_call_target="tpu_custom_call" | custom-call | tf_op jit(solution)/shard_map/attention/pallas_call | solution.py:150
  11.2 2.9 %collective-permute-start.1 = (bf16[32,640]{1,0:T(8,128)(2,1)}, bf16[32,640]{1,0:T(8,128)(2,1)S(1)}, u32[]{:S(2)}, u32[]{:S(2)}) collective-permute-start(bf16[32,640]{1,0:T(8,128)(2,1)} %get-tuple-element.33), channel_id=1, source_target_pairs={{0,8},{4,12},{8,0},{12,4},{16,24},{20,28},{24,16},{28,20},{1,9},{5... | collective-permute-start | bytes 122888 | tf_op jit(solution)/shard_map/ppermute | solution.py:27
  17.0 2.7 %collective-permute-start.5 = (bf16[32,640]{1,0:T(8,128)(2,1)}, bf16[32,640]{1,0:T(8,128)(2,1)S(1)}, u32[]{:S(2)}, u32[]{:S(2)}) collective-permute-start(bf16[32,640]{1,0:T(8,128)(2,1)} %get-tuple-element.37), channel_id=1, source_target_pairs={{0,24},{4,28},{8,16},{12,20},{16,8},{20,12},{24,0},{28,4},{1,25},{... | collective-permute-start | bytes 122888 | tf_op jit(solution)/shard_map/ppermute | solution.py:27
  19.8 2.7 %collective-permute-start.12 = (bf16[80,1280]{1,0:T(8,128)(2,1)S(1)}, bf16[80,1280]{1,0:T(8,128)(2,1)S(1)}, u32[]{:S(2)}, u32[]{:S(2)}) collective-permute-start(bf16[80,1280]{1,0:T(8,128)(2,1)S(1)} %get-tuple-element.81), channel_id=1, source_target_pairs={{0,2},{1,3},{2,0},{3,1},{4,6},{5,7},{6,4},{7,5},{8,10},{9,11},{10,... | collective-permute-start | bytes 614408 | tf_op jit(solution)/shard_map/ppermute | solution.py:27
  22.4 1.6 collective-permute-start.11
  24.0 1.9 %collective-permute-start.13 = (bf16[80,1280]{1,0:T(8,128)(2,1)S(1)}, bf16[80,1280]{1,0:T(8,128)(2,1)S(1)}, u32[]{:S(2)}, u32[]{:S(2)}) collective-permute-start(bf16[80,1280]{1,0:T(8,128)(2,1)S(1)} %get-tuple-element.81), channel_id=1, source_target_pairs={{0,3},{1,2},{2,1},{3,0},{4,7},{5,6},{6,5},{7,4},{8,11},{9,10},{10,... | collective-permute-start | bytes 614408 | tf_op jit(solution)/shard_map/ppermute | solution.py:27
  25.9 1.6 collective-permute-done.20.refs_14_
  29.8 3.3 %collective-permute-done.12 = bf16[80,1280]{1,0:T(8,128)(2,1)S(1)} collective-permute-done((bf16[80,1280]{1,0:T(8,128)(2,1)S(1)}, bf16[80,1280]{1,0:T(8,128)(2,1)S(1)}, u32[]{:S(2)}, u32[]{:S(2)}) %collective-permute-start.12) | collective-permute-done | bytes 204832 | tf_op jit(solution)/shard_map/ppermute | solution.py:27
  33.7 1.6 collective-permute-start.23
  35.3 2.9 %collective-permute-done.13 = bf16[80,1280]{1,0:T(8,128)(2,1)S(1)} collective-permute-done((bf16[80,1280]{1,0:T(8,128)(2,1)S(1)}, bf16[80,1280]{1,0:T(8,128)(2,1)S(1)}, u32[]{:S(2)}, u32[]{:S(2)}) %collective-permute-start.13) | collective-permute-done | bytes 204832 | tf_op jit(solution)/shard_map/ppermute | solution.py:27
  39.1 1.7 %collective-permute-start.25 = (bf16[72,1280]{1,0:T(8,128)(2,1)}, bf16[72,1280]{1,0:T(8,128)(2,1)S(1)}, u32[]{:S(2)}, u32[]{:S(2)}) collective-permute-start(bf16[72,1280]{1,0:T(8,128)(2,1)} %get-tuple-element.47), channel_id=1, source_target_pairs={{0,24},{4,28},{8,16},{12,20},{16,8},{20,12},{24,0},{28,4},{1,25},{... | collective-permute-start | bytes 552968 | tf_op jit(solution)/shard_map/ppermute | solution.py:27
  42.2 3.9 %collective-permute-start.8 = (bf16[256,640]{1,0:T(8,128)(2,1)S(1)}, bf16[256,640]{1,0:T(8,128)(2,1)S(1)}, u32[]{:S(2)}, u32[]{:S(2)}) collective-permute-start(bf16[256,640]{1,0:T(8,128)(2,1)S(1)} %stack_rows.1.refs_0_), channel_id=1, source_target_pairs={{0,1},{1,0},{2,3},{3,2},{4,5},{5,4},{6,7},{7,6},{8,9},{9,8},{10,11... | collective-permute-start | bytes 983048 | tf_op jit(solution)/shard_map/ppermute | solution.py:27
  46.2 7.0 %collective-permute-done.24.refs_18_ = bf16[72,1280]{1,0:T(8,128)(2,1)S(1)} collective-permute-done((bf16[72,1280]{1,0:T(8,128)(2,1)}, bf16[72,1280]{1,0:T(8,128)(2,1)S(1)}, u32[]{:S(2)}, u32[]{:S(2)}) %collective-permute-start.24) | collective-permute-done | bytes 184352 | tf_op jit(solution)/shard_map/ppermute | solution.py:27
  53.1 5.6 %collective-permute-start.7 = (bf16[256,640]{1,0:T(8,128)(2,1)S(1)}, bf16[256,640]{1,0:T(8,128)(2,1)S(1)}, u32[]{:S(2)}, u32[]{:S(2)}) collective-permute-start(bf16[256,640]{1,0:T(8,128)(2,1)S(1)} %stack_rows.1.refs_0_), channel_id=1, source_target_pairs={{0,2},{1,3},{2,0},{3,1},{4,6},{5,7},{6,4},{7,5},{8,10},{9,11},{10,... | collective-permute-start | bytes 983048 | tf_op jit(solution)/shard_map/ppermute | solution.py:27
  64.0 9.8 %collective-permute-done.7.refs_2_ = bf16[256,640]{1,0:T(8,128)(2,1)S(1)} collective-permute-done((bf16[256,640]{1,0:T(8,128)(2,1)S(1)}, bf16[256,640]{1,0:T(8,128)(2,1)S(1)}, u32[]{:S(2)}, u32[]{:S(2)}) %collective-permute-start.7) | collective-permute-done | bytes 327712 | tf_op jit(solution)/shard_map/ppermute | solution.py:27
  77.7 3.1 %fusion = f32[1024]{0:T(1024)S(1)} fusion(bf16[1024,2048]{1,0:T(8,128)(2,1)} %param.12), kind=kLoop, calls=%fused_computation.2 | loop fusion | flops 6290432 | bytes 4198400 | tf_op jit(solution)/shard_map/reduce_sum | solution.py:521
  80.8 7.5 %collective-permute-done.9.refs_3_ = bf16[256,640]{1,0:T(8,128)(2,1)S(1)} collective-permute-done((bf16[256,640]{1,0:T(8,128)(2,1)}, bf16[256,640]{1,0:T(8,128)(2,1)S(1)}, u32[]{:S(2)}, u32[]{:S(2)}) %collective-permute-start.9) | collective-permute-done | bytes 327712 | tf_op jit(solution)/shard_map/ppermute | solution.py:405
  93.0 8.5 %project.1 = (bf16[512,640]{1,0:T(8,128)(2,1)}, bf16[512,640]{1,0:T(8,128)(2,1)}, bf16[128,1024]{1,0:T(8,128)(2,1)}, bf16[128,1024]{1,0:T(8,128)(2,1)}, bf16[128...) custom-call(s32[2]{0:T(128)S(1)} %pad_add_fusion.me, bf16[256,640]{1,0:T(8,128)(2,1)S(1)} %copy-done.4, ...), custom_call_target="tpu_custom_call" | custom-call | tf_op jit(solution)/shard_map/project/pallas_call | solution.py:329
  101.7 1.6 collective-permute-start.28
  110.3 4.7 %collective-permute-done.29 = bf16[128,1024]{1,0:T(8,128)(2,1)S(1)} collective-permute-done((bf16[128,1024]{1,0:T(8,128)(2,1)}, bf16[128,1024]{1,0:T(8,128)(2,1)S(1)}, u32[]{:S(2)}, u32[]{:S(2)}) %collective-permute-start.29) | collective-permute-done | bytes 262176 | tf_op jit(solution)/shard_map/ppermute | solution.py:27
  115.1 1.6 collective-permute-start.30
  116.9 1.6 collective-permute-start.33
  119.3 2.9 %collective-permute-done.30 = bf16[128,1024]{1,0:T(8,128)(2,1)S(1)} collective-permute-done((bf16[128,1024]{1,0:T(8,128)(2,1)S(1)}, bf16[128,1024]{1,0:T(8,128)(2,1)S(1)}, u32[]{:S(2)}, u32[]{:S(2)}) %collective-permute-start.30) | collective-permute-done | bytes 262176 | tf_op jit(solution)/shard_map/ppermute | solution.py:27
  123.9 2.0 %collective-permute-start.36 = (f32[10,128]{1,0:T(8,128)S(1)}, f32[10,128]{1,0:T(8,128)S(1)}, u32[]{:S(2)}, u32[]{:S(2)}) collective-permute-start(f32[10,128]{1,0:T(8,128)S(1)} %maximum_bitcast_fusion), channel_id=1, source_target_pairs={{0,3},{1,2},{2,1},{3,0},{4,7},{5,6},{6,5},{7,4},{8,11},{9,10},{10,... | collective-permute-start | bytes 15368 | tf_op jit(solution)/shard_map/ppermute | solution.py:27
  130.2 1.6 collective-permute-start.44
  134.4 5.0 %collective-permute-done.44.refs_7_ = bf16[128,1024]{1,0:T(8,128)(2,1)S(1)} collective-permute-done((bf16[128,1024]{1,0:T(8,128)(2,1)S(1)}, bf16[128,1024]{1,0:T(8,128)(2,1)S(1)}, u32[]{:S(2)}, u32[]{:S(2)}) %collective-permute-start.44) | collective-permute-done | bytes 262176 | tf_op jit(solution)/shard_map/ppermute | solution.py:27
  142.5 4.1 %collective-permute-done.39.refs_3_ = bf16[128,1024]{1,0:T(8,128)(2,1)S(1)} collective-permute-done((bf16[128,1024]{1,0:T(8,128)(2,1)S(1)}, bf16[128,1024]{1,0:T(8,128)(2,1)S(1)}, u32[]{:S(2)}, u32[]{:S(2)}) %collective-permute-start.39) | collective-permute-done | bytes 262176 | tf_op jit(solution)/shard_map/ppermute | solution.py:27
  148.0 3.4 %collective-permute-done.45.refs_7_ = bf16[128,1024]{1,0:T(8,128)(2,1)S(1)} collective-permute-done((bf16[128,1024]{1,0:T(8,128)(2,1)S(1)}, bf16[128,1024]{1,0:T(8,128)(2,1)S(1)}, u32[]{:S(2)}, u32[]{:S(2)}) %collective-permute-start.45) | collective-permute-done | bytes 262176 | tf_op jit(solution)/shard_map/ppermute | solution.py:27
  151.4 1.9 %collective-permute-done.40.refs_3_ = bf16[128,1024]{1,0:T(8,128)(2,1)S(1)} collective-permute-done((bf16[128,1024]{1,0:T(8,128)(2,1)S(1)}, bf16[128,1024]{1,0:T(8,128)(2,1)S(1)}, u32[]{:S(2)}, u32[]{:S(2)}) %collective-permute-start.40) | collective-permute-done | bytes 262176 | tf_op jit(solution)/shard_map/ppermute | solution.py:27
  153.3 3.4 %fusion.3 = bf16[1024,2048]{1,0:T(8,128)(2,1)} fusion(bf16[1024,2048]{1,0:T(8,128)(2,1)S(1)} %copy-done.24, f32[2048]{0:T(1024)S(1)} %convert_element_type.81, f32[1024]{0:T(1024)S(1)} %fusion.50, pred[1024]{0:T(1024)(128)(4,1)S(1)} %fusion.37, bf16[128,1024]{1,0:T(8,128)(2,1)S(1)} %get-tuple-element.79, bf16[128,1024]{1,0:T(8,128)(2,1)S(1)} %get-tuple-element.78, ...), kind=kOutput, calls=%fused_computation.5 | convolution fusion | flops 548536320 | bytes 8926720 | tf_op jit(solution)/shard_map/dot_general | solution.py:18
  157.5 2.4 %shard_map.104.refs_10_ = f32[640,2048]{1,0:T(8,128)S(1)} custom-call(bf16[640,512]{1,0:T(8,128)(2,1)S(1)} %get-tuple-element.58.refs_0_, bf16[640,512]{1,0:T(8,128)(2,1)S(1)} %get-tuple-element.59.refs_1_, bf16[128,1024]{1,0:T(8,128)(2,1)S(1)} %get-tuple-element.69.refs_2_, bf16[128,1024]{1,0:T(8,128)(2,1)S(1)} %collective-permute-done.39.refs_3_, ...), custom_call_target="tpu_custom_call" | custom-call | tf_op jit(solution)/shard_map/pallas_call | solution.py:389
  159.9 4.0 %shard_map.105 = f32[640,2048]{1,0:T(8,128)} custom-call(bf16[640,512]{1,0:T(8,128)(2,1)S(1)} %get-tuple-element.56.refs_0_, bf16[640,512]{1,0:T(8,128)(2,1)S(1)} %get-tuple-element.57.refs_1_, bf16[128,1024]{1,0:T(8,128)(2,1)S(1)} %collective-permute-done.38.refs_2_, bf16[128,1024]{1,0:T(8,128)(2,1)S(1)} %collective-permute-done.40.refs_3_, ...), custom_call_target="tpu_custom_call" | custom-call | tf_op jit(solution)/shard_map/pallas_call | solution.py:389
  (163 shorter events, 44.2 us)
Async XLA Ops:
  0.6 87.7 %collective-permute-start.27 = (bf16[640,2048]{1,0:T(8,128)(2,1)}, bf16[640,2048]{1,0:T(8,128)(2,1)S(1)}, u32[]{:S(2)}, u32[]{:S(2)}) collective-permute-start(bf16[640,2048]{1,0:T(8,128)(2,1)} %refs_21_.1), channel_id=1, source_target_pairs={{0,4},{4,0},{8,12},{12,8},{16,20},{20,16},{24,28},{28,24},{1,5},{5... | collective-permute-start | bytes 7864328 | tf_op jit(solution)/shard_map/ppermute | solution.py:27
  19.8 13.4 %collective-permute-start.12 = (bf16[80,1280]{1,0:T(8,128)(2,1)S(1)}, bf16[80,1280]{1,0:T(8,128)(2,1)S(1)}, u32[]{:S(2)}, u32[]{:S(2)}) collective-permute-start(bf16[80,1280]{1,0:T(8,128)(2,1)S(1)} %get-tuple-element.81), channel_id=1, source_target_pairs={{0,2},{1,3},{2,0},{3,1},{4,6},{5,7},{6,4},{7,5},{8,10},{9,11},{10,... | collective-permute-start | bytes 614408 | tf_op jit(solution)/shard_map/ppermute | solution.py:27
  22.4 11.2 %collective-permute-start.11 = (bf16[80,1280]{1,0:T(8,128)(2,1)S(1)}, bf16[80,1280]{1,0:T(8,128)(2,1)S(1)}, u32[]{:S(2)}, u32[]{:S(2)}) collective-permute-start(bf16[80,1280]{1,0:T(8,128)(2,1)S(1)} %get-tuple-element.81), channel_id=1, source_target_pairs={{0,1},{1,0},{2,3},{3,2},{4,5},{5,4},{6,7},{7,6},{8,9},{9,8},{10,11... | collective-permute-start | bytes 614408 | tf_op jit(solution)/shard_map/ppermute | solution.py:27
  24.0 14.2 %collective-permute-start.13 = (bf16[80,1280]{1,0:T(8,128)(2,1)S(1)}, bf16[80,1280]{1,0:T(8,128)(2,1)S(1)}, u32[]{:S(2)}, u32[]{:S(2)}) collective-permute-start(bf16[80,1280]{1,0:T(8,128)(2,1)S(1)} %get-tuple-element.81), channel_id=1, source_target_pairs={{0,3},{1,2},{2,1},{3,0},{4,7},{5,6},{6,5},{7,4},{8,11},{9,10},{10,... | collective-permute-start | bytes 614408 | tf_op jit(solution)/shard_map/ppermute | solution.py:27
  28.2 10.9 %collective-permute-start.21 = (bf16[72,1280]{1,0:T(8,128)(2,1)}, bf16[72,1280]{1,0:T(8,128)(2,1)S(1)}, u32[]{:S(2)}, u32[]{:S(2)}) collective-permute-start(bf16[72,1280]{1,0:T(8,128)(2,1)} %get-tuple-element.43), channel_id=1, source_target_pairs={{0,8},{4,12},{8,0},{12,4},{16,24},{20,28},{24,16},{28,20},{1,9},{5... | collective-permute-start | bytes 552968 | tf_op jit(solution)/shard_map/ppermute | solution.py:27
  33.7 8.6 %collective-permute-start.23 = (bf16[72,1280]{1,0:T(8,128)(2,1)}, bf16[72,1280]{1,0:T(8,128)(2,1)S(1)}, u32[]{:S(2)}, u32[]{:S(2)}) collective-permute-start(bf16[72,1280]{1,0:T(8,128)(2,1)} %get-tuple-element.45), channel_id=1, source_target_pairs={{0,16},{4,20},{8,24},{12,28},{16,0},{20,4},{24,8},{28,12},{1,17},{... | collective-permute-start | bytes 552968 | tf_op jit(solution)/shard_map/ppermute | solution.py:27
  38.2 15.0 %collective-permute-start.24 = (bf16[72,1280]{1,0:T(8,128)(2,1)}, bf16[72,1280]{1,0:T(8,128)(2,1)S(1)}, u32[]{:S(2)}, u32[]{:S(2)}) collective-permute-start(bf16[72,1280]{1,0:T(8,128)(2,1)} %get-tuple-element.46), channel_id=1, source_target_pairs={{0,20},{4,16},{8,28},{12,24},{16,4},{20,0},{24,12},{28,8},{1,21},{... | collective-permute-start | bytes 552968 | tf_op jit(solution)/shard_map/ppermute | solution.py:27
  39.1 19.7 %collective-permute-start.25 = (bf16[72,1280]{1,0:T(8,128)(2,1)}, bf16[72,1280]{1,0:T(8,128)(2,1)S(1)}, u32[]{:S(2)}, u32[]{:S(2)}) collective-permute-start(bf16[72,1280]{1,0:T(8,128)(2,1)} %get-tuple-element.47), channel_id=1, source_target_pairs={{0,24},{4,28},{8,16},{12,20},{16,8},{20,12},{24,0},{28,4},{1,25},{... | collective-permute-start | bytes 552968 | tf_op jit(solution)/shard_map/ppermute | solution.py:27
  40.9 20.2 %collective-permute-start.26 = (bf16[72,1280]{1,0:T(8,128)(2,1)}, bf16[72,1280]{1,0:T(8,128)(2,1)S(1)}, u32[]{:S(2)}, u32[]{:S(2)}) collective-permute-start(bf16[72,1280]{1,0:T(8,128)(2,1)} %get-tuple-element.48), channel_id=1, source_target_pairs={{0,28},{4,24},{8,20},{12,16},{16,12},{20,8},{24,4},{28,0},{1,29},{... | collective-permute-start | bytes 552968 | tf_op jit(solution)/shard_map/ppermute | solution.py:27
  42.2 21.0 %collective-permute-start.8 = (bf16[256,640]{1,0:T(8,128)(2,1)S(1)}, bf16[256,640]{1,0:T(8,128)(2,1)S(1)}, u32[]{:S(2)}, u32[]{:S(2)}) collective-permute-start(bf16[256,640]{1,0:T(8,128)(2,1)S(1)} %stack_rows.1.refs_0_), channel_id=1, source_target_pairs={{0,1},{1,0},{2,3},{3,2},{4,5},{5,4},{6,7},{7,6},{8,9},{9,8},{10,11... | collective-permute-start | bytes 983048 | tf_op jit(solution)/shard_map/ppermute | solution.py:27
  53.1 20.6 %collective-permute-start.7 = (bf16[256,640]{1,0:T(8,128)(2,1)S(1)}, bf16[256,640]{1,0:T(8,128)(2,1)S(1)}, u32[]{:S(2)}, u32[]{:S(2)}) collective-permute-start(bf16[256,640]{1,0:T(8,128)(2,1)S(1)} %stack_rows.1.refs_0_), channel_id=1, source_target_pairs={{0,2},{1,3},{2,0},{3,1},{4,6},{5,7},{6,4},{7,5},{8,10},{9,11},{10,... | collective-permute-start | bytes 983048 | tf_op jit(solution)/shard_map/ppermute | solution.py:27
  59.5 15.1 %collective-permute-start.17 = (bf16[4,80,640]{2,1,0:T(8,128)(2,1)S(1)}, bf16[4,80,640]{2,1,0:T(8,128)(2,1)}, u32[]{:S(2)}, u32[]{:S(2)}) collective-permute-start(bf16[4,80,640]{2,1,0:T(8,128)(2,1)S(1)} %get-tuple-element.70.refs_9_), channel_id=1, source_target_pairs={{0,8},{4,12},{8,0},{12,4},{16,24},{20,28},{24,16},{28,20},{1,9},{5... | collective-permute-start | bytes 1228808 | tf_op jit(solution)/shard_map/ppermute | solution.py:27
  61.7 13.4 %collective-permute-start.14 = (bf16[4,80,640]{2,1,0:T(8,128)(2,1)S(1)}, bf16[4,80,640]{2,1,0:T(8,128)(2,1)}, u32[]{:S(2)}, u32[]{:S(2)}) collective-permute-start(bf16[4,80,640]{2,1,0:T(8,128)(2,1)S(1)} %get-tuple-element.71.refs_5_), channel_id=1, source_target_pairs={{0,16},{4,20},{8,24},{12,28},{16,0},{20,4},{24,8},{28,12},{1,17},{... | collective-permute-start | bytes 1228808 | tf_op jit(solution)/shard_map/ppermute | solution.py:27
  64.0 11.3 %collective-permute-start.18 = (bf16[4,80,640]{2,1,0:T(8,128)(2,1)S(1)}, bf16[4,80,640]{2,1,0:T(8,128)(2,1)}, u32[]{:S(2)}, u32[]{:S(2)}) collective-permute-start(bf16[4,80,640]{2,1,0:T(8,128)(2,1)S(1)} %get-tuple-element.70.refs_9_), channel_id=1, source_target_pairs={{0,4},{4,0},{8,12},{12,8},{16,20},{20,16},{24,28},{28,24},{1,5},{5... | collective-permute-start | bytes 1228808 | tf_op jit(solution)/shard_map/ppermute | solution.py:27
  74.6 13.7 %collective-permute-start.19 = (bf16[4,80,640]{2,1,0:T(8,128)(2,1)}, bf16[4,80,640]{2,1,0:T(8,128)(2,1)S(1)}, u32[]{:S(2)}, u32[]{:S(2)}) collective-permute-start(bf16[4,80,640]{2,1,0:T(8,128)(2,1)} %collective-permute-done.17.refs_10_), channel_id=1, source_target_pairs={{0,4},{4,0},{8,12},{12,8},{16,20},{20,16},{24,28},{28,24},{1,5},{5... | collective-permute-start | bytes 1228808 | tf_op jit(solution)/shard_map/ppermute | solution.py:27
  75.2 13.2 %collective-permute-start.16 = (bf16[4,80,640]{2,1,0:T(8,128)(2,1)}, bf16[4,80,640]{2,1,0:T(8,128)(2,1)S(1)}, u32[]{:S(2)}, u32[]{:S(2)}) collective-permute-start(bf16[4,80,640]{2,1,0:T(8,128)(2,1)} %collective-permute-done.14.refs_6_), channel_id=1, source_target_pairs={{0,4},{4,0},{8,12},{12,8},{16,20},{20,16},{24,28},{28,24},{1,5},{5... | collective-permute-start | bytes 1228808 | tf_op jit(solution)/shard_map/ppermute | solution.py:27
  76.4 11.9 %collective-permute-start.9 = (bf16[256,640]{1,0:T(8,128)(2,1)}, bf16[256,640]{1,0:T(8,128)(2,1)S(1)}, u32[]{:S(2)}, u32[]{:S(2)}) collective-permute-start(bf16[256,640]{1,0:T(8,128)(2,1)} %copy-done.7), channel_id=1, source_target_pairs={{1,0},{2,3},{5,4},{6,7},{9,8},{10,11},{13,12},{14,15},{17,16},{18,... | collective-permute-start | bytes 983048 | tf_op jit(solution)/shard_map/ppermute | solution.py:405
  101.7 17.6 %collective-permute-start.28 = (bf16[128,1024]{1,0:T(8,128)(2,1)}, bf16[128,1024]{1,0:T(8,128)(2,1)S(1)}, u32[]{:S(2)}, u32[]{:S(2)}) collective-permute-start(bf16[128,1024]{1,0:T(8,128)(2,1)} %get-tuple-element.52), channel_id=1, source_target_pairs={{0,8},{4,12},{8,0},{12,4},{16,24},{20,28},{24,16},{28,20},{1,9},{5... | collective-permute-start | bytes 786440 | tf_op jit(solution)/shard_map/ppermute | solution.py:27
  103.3 11.8 %collective-permute-start.29 = (bf16[128,1024]{1,0:T(8,128)(2,1)}, bf16[128,1024]{1,0:T(8,128)(2,1)S(1)}, u32[]{:S(2)}, u32[]{:S(2)}) collective-permute-start(bf16[128,1024]{1,0:T(8,128)(2,1)} %get-tuple-element.53), channel_id=1, source_target_pairs={{0,8},{4,12},{8,0},{12,4},{16,24},{20,28},{24,16},{28,20},{1,9},{5... | collective-permute-start | bytes 786440 | tf_op jit(solution)/shard_map/ppermute | solution.py:27
  103.7 15.6 %collective-permute-start.31 = (bf16[128,1024]{1,0:T(8,128)(2,1)}, bf16[128,1024]{1,0:T(8,128)(2,1)S(1)}, u32[]{:S(2)}, u32[]{:S(2)}) collective-permute-start(bf16[128,1024]{1,0:T(8,128)(2,1)} %get-tuple-element.54), channel_id=1, source_target_pairs={{0,16},{4,20},{8,24},{12,28},{16,0},{20,4},{24,8},{28,12},{1,17},{... | collective-permute-start | bytes 786440 | tf_op jit(solution)/shard_map/ppermute | solution.py:27
  105.3 11.6 %collective-permute-start.32 = (bf16[128,1024]{1,0:T(8,128)(2,1)}, bf16[128,1024]{1,0:T(8,128)(2,1)S(1)}, u32[]{:S(2)}, u32[]{:S(2)}) collective-permute-start(bf16[128,1024]{1,0:T(8,128)(2,1)} %get-tuple-element.55), channel_id=1, source_target_pairs={{0,16},{4,20},{8,24},{12,28},{16,0},{20,4},{24,8},{28,12},{1,17},{... | collective-permute-start | bytes 786440 | tf_op jit(solution)/shard_map/ppermute | solution.py:27
  130.2 9.2 %collective-permute-start.44 = (bf16[128,1024]{1,0:T(8,128)(2,1)S(1)}, bf16[128,1024]{1,0:T(8,128)(2,1)S(1)}, u32[]{:S(2)}, u32[]{:S(2)}) collective-permute-start(bf16[128,1024]{1,0:T(8,128)(2,1)S(1)} %get-tuple-element.68.refs_6_), channel_id=1, source_target_pairs={{0,8},{4,12},{8,0},{12,4},{16,24},{20,28},{24,16},{28,20},{1,9},{5... | collective-permute-start | bytes 786440 | tf_op jit(solution)/shard_map/ppermute | solution.py:27
  131.8 9.2 %collective-permute-start.43 = (bf16[128,1024]{1,0:T(8,128)(2,1)S(1)}, bf16[128,1024]{1,0:T(8,128)(2,1)S(1)}, u32[]{:S(2)}, u32[]{:S(2)}) collective-permute-start(bf16[128,1024]{1,0:T(8,128)(2,1)S(1)} %get-tuple-element.68.refs_6_), channel_id=1, source_target_pairs={{0,16},{4,20},{8,24},{12,28},{16,0},{20,4},{24,8},{28,12},{1,17},{... | collective-permute-start | bytes 786440 | tf_op jit(solution)/shard_map/ppermute | solution.py:27
  133.3 13.3 %collective-permute-start.39 = (bf16[128,1024]{1,0:T(8,128)(2,1)S(1)}, bf16[128,1024]{1,0:T(8,128)(2,1)S(1)}, u32[]{:S(2)}, u32[]{:S(2)}) collective-permute-start(bf16[128,1024]{1,0:T(8,128)(2,1)S(1)} %get-tuple-element.69.refs_2_), channel_id=1, source_target_pairs={{0,16},{4,20},{8,24},{12,28},{16,0},{20,4},{24,8},{28,12},{1,17},{... | collective-permute-start | bytes 786440 | tf_op jit(solution)/shard_map/ppermute | solution.py:27
  133.8 13.5 %collective-permute-start.48 = (bf16[128,1024]{1,0:T(8,128)(2,1)S(1)}, bf16[128,1024]{1,0:T(8,128)(2,1)S(1)}, u32[]{:S(2)}, u32[]{:S(2)}) collective-permute-start(bf16[128,1024]{1,0:T(8,128)(2,1)S(1)} %get-tuple-element.69.refs_2_), channel_id=1, source_target_pairs={{0,4},{4,0},{8,12},{12,8},{16,20},{20,16},{24,28},{28,24},{1,5},{5... | collective-permute-start | bytes 786440 | tf_op jit(solution)/shard_map/ppermute | solution.py:27
  133.8 13.6 %collective-permute-start.38 = (bf16[128,1024]{1,0:T(8,128)(2,1)S(1)}, bf16[128,1024]{1,0:T(8,128)(2,1)S(1)}, u32[]{:S(2)}, u32[]{:S(2)}) collective-permute-start(bf16[128,1024]{1,0:T(8,128)(2,1)S(1)} %get-tuple-element.69.refs_2_), channel_id=1, source_target_pairs={{0,8},{4,12},{8,0},{12,4},{16,24},{20,28},{24,16},{28,20},{1,9},{5... | collective-permute-start | bytes 786440 | tf_op jit(solution)/shard_map/ppermute | solution.py:27
  139.4 8.5 %collective-permute-start.51 = (bf16[128,1024]{1,0:T(8,128)(2,1)S(1)}, bf16[128,1024]{1,0:T(8,128)(2,1)S(1)}, u32[]{:S(2)}, u32[]{:S(2)}) collective-permute-start(bf16[128,1024]{1,0:T(8,128)(2,1)S(1)} %collective-permute-done.44.refs_7_), channel_id=1, source_target_pairs={{0,4},{4,0},{8,12},{12,8},{16,20},{20,16},{24,28},{28,24},{1,5},{5... | collective-permute-start | bytes 786440 | tf_op jit(solution)/shard_map/ppermute | solution.py:27
  141.0 10.4 %collective-permute-start.45 = (bf16[128,1024]{1,0:T(8,128)(2,1)S(1)}, bf16[128,1024]{1,0:T(8,128)(2,1)S(1)}, u32[]{:S(2)}, u32[]{:S(2)}) collective-permute-start(bf16[128,1024]{1,0:T(8,128)(2,1)S(1)} %collective-permute-done.44.refs_7_), channel_id=1, source_target_pairs={{0,16},{4,20},{8,24},{12,28},{16,0},{20,4},{24,8},{28,12},{1,17},{... | collective-permute-start | bytes 786440 | tf_op jit(solution)/shard_map/ppermute | solution.py:27
  147.3 10.2 %collective-permute-start.49 = (bf16[128,1024]{1,0:T(8,128)(2,1)S(1)}, bf16[128,1024]{1,0:T(8,128)(2,1)S(1)}, u32[]{:S(2)}, u32[]{:S(2)}) collective-permute-start(bf16[128,1024]{1,0:T(8,128)(2,1)S(1)} %collective-permute-done.39.refs_3_), channel_id=1, source_target_pairs={{0,4},{4,0},{8,12},{12,8},{16,20},{20,16},{24,28},{28,24},{1,5},{5... | collective-permute-start | bytes 786440 | tf_op jit(solution)/shard_map/ppermute | solution.py:27
  147.4 12.5 %collective-permute-start.46 = (bf16[128,1024]{1,0:T(8,128)(2,1)S(1)}, bf16[128,1024]{1,0:T(8,128)(2,1)S(1)}, u32[]{:S(2)}, u32[]{:S(2)}) collective-permute-start(bf16[128,1024]{1,0:T(8,128)(2,1)S(1)} %collective-permute-done.43.refs_6_), channel_id=1, source_target_pairs={{0,4},{4,0},{8,12},{12,8},{16,20},{20,16},{24,28},{28,24},{1,5},{5... | collective-permute-start | bytes 786440 | tf_op jit(solution)/shard_map/ppermute | solution.py:27
  147.9 12.0 %collective-permute-start.41 = (bf16[128,1024]{1,0:T(8,128)(2,1)S(1)}, bf16[128,1024]{1,0:T(8,128)(2,1)S(1)}, u32[]{:S(2)}, u32[]{:S(2)}) collective-permute-start(bf16[128,1024]{1,0:T(8,128)(2,1)S(1)} %collective-permute-done.38.refs_2_), channel_id=1, source_target_pairs={{0,4},{4,0},{8,12},{12,8},{16,20},{20,16},{24,28},{28,24},{1,5},{5... | collective-permute-start | bytes 786440 | tf_op jit(solution)/shard_map/ppermute | solution.py:27
  151.4 8.5 %collective-permute-start.47 = (bf16[128,1024]{1,0:T(8,128)(2,1)S(1)}, bf16[128,1024]{1,0:T(8,128)(2,1)S(1)}, u32[]{:S(2)}, u32[]{:S(2)}) collective-permute-start(bf16[128,1024]{1,0:T(8,128)(2,1)S(1)} %collective-permute-done.45.refs_7_), channel_id=1, source_target_pairs={{0,4},{4,0},{8,12},{12,8},{16,20},{20,16},{24,28},{28,24},{1,5},{5... | collective-permute-start | bytes 786440 | tf_op jit(solution)/shard_map/ppermute | solution.py:27
  (48 other events, 501.3 us)
